TPU v7x, 32 devices: a whole 2x2x4 slice. The times are simulated.
32 devices in a mesh: narrow: 4 (over y, x), wide: 8 (over z, core).
Axes of the slice: x: 2, y: 2, z: 4, core: 2. Of those that a mesh axis runs over, the one named last changes fastest.
Arguments:
- level_set: float32 [256, 256, 512], P('wide', 'narrow')
- velocity: bfloat16 [3, 256, 256, 512], P(None, 'wide', 'narrow'), may hold values from -2 to 2
- box_owner: int32 [8, 4, 256, 1], P('wide', 'narrow'), may hold values from 0 to 7; in each aligned block of 256 rows (0 to 255, 256 to 511, ..., all dimensions but the last counted through in order) at most 80 rows name the same one
Outputs:
- surface: float32 [256, 256, 512], P('wide', 'narrow')
- box_fractions: float32 [8, 4, 640, 512], P('wide', 'narrow')
Inputs may be any that keep to these rules, and one draw needn't show every extreme that they name: `box_owner`: the tiles of one device name one box owner at most 80 times.
All inputs are finite; a program needn't handle non-finite values.
Results may differ from a plain program's by a relative error of at most 0.0003.
Values sent between devices are 32-bit elements; how exact they have to be, the bound alone decides.
No kernel may reach another device: no remote copies, remote signals or barrier semaphores. Data moves between devices by JAX's collectives and lax.ppermute only.
A program may use at most 192 MiB of HBM per device.

v0:
```python
import functools
import math
import jax
import jax.numpy as jnp
import numpy as np
from jax import lax
from jax.experimental import pallas as pl
from jax.experimental.pallas import tpu as pltpu
from jax.sharding import PartitionSpec as P

TILE = 16
WENO_EPS = 1e-06
PSEUDO_STEP = 0.3
RIM = 3
SECOND = 12
LANES = 128
ROWS = 8
MIB = 1024 * 1024


def correction(s1, s2, s3, h1, h0):
    r1 = 1.0 / s1
    r2 = 1.0 / s2
    r3 = 1.0 / s3
    w1 = (r1 * r1) * (1.0 / 3.0)
    w2 = (r2 * r2) * 2.0
    w3 = r3 * r3
    return (w1 * (4.0 * h1 - h0) + (w3 - w2) * h0) / ((w1 + w3) + w2)


def pair_forms(x, y, t):
    t2 = t + t
    q = t * t + 0.75 * WENO_EPS
    y75 = 0.75 * y
    w = q + y75 * x
    u = w + y75 * t2
    v = w - (0.75 * x) * t2
    return u, w, v


def rolled(chunks, shift, fill):
    lane = lax.broadcasted_iota(jnp.int32, chunks[0].shape, 1)
    turned = [pltpu.roll(c, (-shift) % LANES, 1) for c in chunks]
    out = []
    n = len(chunks)
    for k in range(n):
        other = k + (1 if shift > 0 else -1)
        beyond = turned[other] if 0 <= other < n else fill(k)
        mask = lane >= LANES - shift if shift > 0 else lane < -shift
        out.append(jnp.where(mask, beyond, turned[k]))
    return out


def along_z_kernel(core, u_hbm, field, acc, u, uz, sem):
    nx, ny, nz = core.shape
    copies = Copies(sem)
    bounds = [0, nx // 16, nx // 4, nx // 2, 3 * nx // 4, nx]
    groups = list(zip(bounds, bounds[1:]))
    for x0, x1 in groups:
        xs = pl.ds(x0, x1 - x0)
        for k, lanes in lane_chunks(nz):
            copies.start(x0, core.at[xs, :, lanes], field.at[pl.ds(x0 + RIM, x1 - x0), k, pl.ds(ROWS, ny), :])
        copies.start(x0, u_hbm.at[2, xs], uz.at[xs])
    copies.start("u", u_hbm.at[pl.ds(0, 2)], u)
    for x0, x1 in groups:
        copies.wait(x0)
        lax.fori_loop(x0, x1, functools.partial(z_plane, field, uz, acc, ny, nz), 0)
    copies.finish()


def z_plane(field, uz, acc, rows, depth, x, carry):
    n = depth // LANES
    zero = jnp.zeros((ROWS, LANES), jnp.float32)
    eps = 0.75 * WENO_EPS
    for yb in range(rows // ROWS):
        ys = pl.ds(yb * ROWS, ROWS)
        yf = pl.ds(yb * ROWS + ROWS, ROWS)
        f = [field[x + RIM, k, yf, :] for k in range(n)]
        fp = rolled(f, 1, lambda k: f[k])
        fm = rolled(f, -1, lambda k: f[k])
        e = [(fp[k] - f[k]) - (f[k] - fm[k]) for k in range(n)]
        ep = rolled(e, 1, lambda k: zero)
        em = rolled(e, -1, lambda k: zero)
        epp = rolled(e, 2, lambda k: zero)
        emm = rolled(e, -2, lambda k: zero)
        for k in range(n):
            v = uz[x, ys, pl.ds(k * LANES, LANES)].astype(jnp.float32)
            up = v > 0
            c = e[k]
            a = jnp.where(up, emm[k], epp[k])
            b = jnp.where(up, em[k], ep[k])
            d = jnp.where(up, ep[k], em[k])
            al, be, ga = b - a, c - b, d - c
            b75, c75 = 0.75 * b, 0.75 * c
            s1 = (al * al + eps) + b75 * (b + al)
            s2 = (be * be + eps) + b75 * c
            s3 = (ga * ga + eps) + c75 * (c - ga)
            phi = correction(s1, s2, s3, be - al, ga - be)
            mid = 6.0 * (fp[k] - fm[k]) - (ep[k] - em[k])
            v12 = v * (1.0 / 12.0)
            acc[x + RIM, k, yf, :] = f[k] - (v12 * mid - jnp.abs(v12) * phi)
    return carry


def in_vmem(shape, dtype=jnp.float32):
    return pltpu.VMEM(shape, dtype)


def rimmed(shape):
    nx, ny, nz = shape
    return in_vmem((nx + 2 * RIM, nz // LANES, ny + 2 * ROWS, LANES))


def along_z(level_set, velocity):
    nx, ny, nz = level_set.shape
    return pl.pallas_call(
        along_z_kernel,
        in_specs=[ANY, ANY],
        out_specs=[INSIDE] * 3,
        out_shape=[rimmed(level_set.shape)] * 2 + [in_vmem((2, nx, ny, nz), velocity.dtype)],
        scratch_shapes=[pltpu.VMEM((nx, ny, nz), velocity.dtype), pltpu.SemaphoreType.DMA((40,))],
        name="along_z",
        cost_estimate=estimate(level_set, 60),
        compiler_params=pltpu.CompilerParams(vmem_limit_bytes=46 * MIB),
    )(level_set, velocity)


def estimate(block, flops):
    return pl.CostEstimate(flops=flops * block.size, bytes_accessed=8 * block.size, transcendentals=4 * block.size)


class Copies:
    def __init__(self, sem):
        self.sem, self.used, self.groups = sem, 0, {}

    def start(self, group, src, dst):
        copy = pltpu.make_async_copy(src, dst, self.sem.at[self.used])
        self.used += 1
        copy.start()
        self.groups.setdefault(group, []).append(copy)

    def wait(self, group):
        for copy in self.groups.pop(group, ()):
            copy.wait()

    def finish(self):
        for group in list(self.groups):
            self.wait(group)


def lane_chunks(nz):
    return [(k, pl.ds(k * LANES, LANES)) for k in range(nz // LANES)]


def x_column(field, u, acc, k, yb, ranges):
    ys = pl.ds(pl.multiple_of(yb * ROWS, ROWS), ROWS)
    yf = pl.ds(pl.multiple_of(yb * ROWS + ROWS, ROWS), ROWS)
    lanes = pl.ds(pl.multiple_of(k * LANES, LANES), LANES)
    for first, last in ranges:
        f, g, e, t, h, pu, pw, pv = {}, {}, {}, {}, {}, {}, {}, {}

        def value(x):
            f[x] = field[x + RIM, k, yf, :]
            if x - 1 in f:
                g[x - 1] = f[x] - f[x - 1]
            if x - 2 in g:
                e[x - 1] = g[x - 1] - g[x - 2]
            if x - 2 in e:
                t[x - 2] = e[x - 1] - e[x - 2]
                pu[x - 2], pw[x - 2], pv[x - 2] = pair_forms(e[x - 2], e[x - 1], t[x - 2])
            if x - 3 in t:
                h[x - 2] = t[x - 2] - t[x - 3]

        for x in range(first - RIM, first + RIM):
            value(x)
        for x in range(first, last):
            value(x + RIM)
            v = u[0, x, ys, lanes].astype(jnp.float32)
            up = v > 0
            s1 = jnp.where(up, pu[x - 2], pv[x + 1])
            s2 = jnp.where(up, pw[x - 1], pw[x])
            s3 = jnp.where(up, pv[x], pu[x - 1])
            h1 = jnp.where(up, h[x - 1], h[x + 1])
            phi = correction(s1, s2, s3, h1, h[x])
            mid = 6.0 * (g[x] + g[x - 1]) - (e[x + 1] - e[x - 1])
            v12 = v * (1.0 / 12.0)
            acc[x + RIM, k, yf, :] = acc[x + RIM, k, yf, :] - (v12 * mid - jnp.abs(v12) * phi)


def y_plane(field, u, acc, streams, x, n, ranges):
    es, us, ws, vs, hs = streams
    for k in range(n):
        lanes = pl.ds(k * LANES, LANES)

        def at(y):
            return field[x + RIM, k, pl.ds(ROWS + y, ROWS), :]

        for first, last in ranges:
            for b in range(first, last + 1):
                y = b * ROWS - 2
                f0 = at(y)
                es[k, pl.ds(ROWS + b * ROWS, ROWS), :] = (at(y + 1) - f0) - (f0 - at(y - 1))
            for b in range(first, last + 1):
                r = ROWS + b * ROWS
                e0, e1, e_1 = es[k, pl.ds(r, ROWS), :], es[k, pl.ds(r + 1, ROWS), :], es[k, pl.ds(r - 1, ROWS), :]
                t = e1 - e0
                us[k, pl.ds(r, ROWS), :], ws[k, pl.ds(r, ROWS), :], vs[k, pl.ds(r, ROWS), :] = pair_forms(e0, e1, t)
                hs[k, pl.ds(r, ROWS), :] = t - (e0 - e_1)
            for b in range(first, last):
                ys, yf = pl.ds(b * ROWS, ROWS), pl.ds(b * ROWS + ROWS, ROWS)

                def of(ref, d):
                    return ref[k, pl.ds(ROWS + b * ROWS + 2 + d, ROWS), :]

                v = u[1, x, ys, lanes].astype(jnp.float32)
                up = v > 0
                s1 = jnp.where(up, of(us, -2), of(vs, 1))
                s2 = jnp.where(up, of(ws, -1), of(ws, 0))
                s3 = jnp.where(up, of(vs, 0), of(us, -1))
                h1 = jnp.where(up, of(hs, -1), of(hs, 1))
                phi = correction(s1, s2, s3, h1, of(hs, 0))
                mid = 6.0 * (at(b * ROWS + 1) - at(b * ROWS - 1)) - (of(es, 1) - of(es, -1))
                v12 = v * (1.0 / 12.0)
                acc[x + RIM, k, yf, :] = acc[x + RIM, k, yf, :] - (v12 * mid - jnp.abs(v12) * phi)


def place_rows(field, x0, count, upper, first, second, ny, second_at=0):
    n = field.shape[1]

    def body(i, carry):
        for k in range(n):
            one = first[k, pl.ds(RIM * i, RIM), :]
            two = second[k, pl.ds(second_at + RIM * i, RIM), :]
            field[i + x0, k, pl.ds(ROWS - RIM, RIM), :] = jnp.where(upper, two, one)
            field[i + x0, k, pl.ds(ROWS + ny, RIM), :] = jnp.where(upper, one, two)
        return carry

    lax.fori_loop(0, count, body, 0)


def side_shape(shape):
    nx, _, nz = shape
    return (nz // LANES, RIM * nx, LANES)


def first_is_above(axis):
    return lax.rem(lax.axis_index(axis), 2) == 0


def face_starts(nx):
    even = first_is_above("wide")
    faces = (jnp.where(even, nx - RIM, 0), jnp.where(even, 0, nx - RIM))
    rims = (jnp.where(even, nx + RIM, 0), jnp.where(even, 0, nx + RIM))
    return faces, rims


def pieces(nx):
    count = math.gcd(nx, 4)
    return [(i * (nx // count), nx // count) for i in range(count)]


def edge_rows_kernel(
    field_in, acc_in, u, xa, xb, ya_hbm, yb_hbm, field, acc, yfa_hbm, yfb_hbm, es, us, ws, vs, hs, ya, yb, yf_a, yf_b, sem
):
    _, nx, ny, nz = u.shape
    n, nb = nz // LANES, ny // ROWS
    copies = Copies(sem)
    streams = (es, us, ws, vs, hs)
    _, rims = face_starts(nx)
    upper = first_is_above("narrow")
    for block, rim in zip((xa, xb), rims):
        for k, lanes in lane_chunks(nz):
            copies.start("x", block.at[:, :, lanes], field.at[pl.ds(rim, RIM), k, pl.ds(ROWS, ny), :])
    copies.start("y", ya_hbm, ya)
    copies.start("y", yb_hbm, yb)
    copies.wait("x")

    def edge_column(i, carry):
        x_column(field, u, acc, lax.rem(i, n), lax.div(i, n) * (nb - 1), ((0, nx),))
        return carry

    lax.fori_loop(0, 2 * n, edge_column, 0)
    copies.wait("y")
    place_rows(field, RIM, nx, upper, ya, yb, ny)

    def edge_plane(x, carry):
        y_plane(field, u, acc, streams, x, n, ((0, 1), (nb - 1, nb)))
        for k in range(n):
            lo, hi = acc[x + RIM, k, pl.ds(ROWS, RIM), :], acc[x + RIM, k, pl.ds(ROWS + ny - RIM, RIM), :]
            yf_a[k, pl.ds(RIM * x, RIM), :] = jnp.where(upper, hi, lo)
            yf_b[k, pl.ds(RIM * x, RIM), :] = jnp.where(upper, lo, hi)
        return carry

    for x0, count in pieces(nx):
        rows = pl.ds(RIM * x0, RIM * count)
        lax.fori_loop(x0, x0 + count, edge_plane, 0)
        copies.start("out", yf_a.at[:, rows], yfa_hbm.at[:, rows])
        copies.start("out", yf_b.at[:, rows], yfb_hbm.at[:, rows])
    copies.finish()


def edge_planes_kernel(acc_in, field, u, acc, bx_a, bx_b, es, us, ws, vs, hs, sem):
    _, nx, ny, nz = u.shape
    n, nb = nz // LANES, ny // ROWS
    copies = Copies(sem)
    faces, _ = face_starts(nx)

    def both_ends(i, carry):
        y_plane(field, u, acc, (es, us, ws, vs, hs), jnp.where(i < RIM, i, nx - 2 * RIM + i), n, ((1, nb - 1),))
        return carry

    lax.fori_loop(0, 2 * RIM, both_ends, 0)

    def inner_column(i, carry):
        x_column(field, u, acc, lax.rem(i, n), 1 + lax.div(i, n), ((0, RIM), (nx - RIM, nx)))
        return carry

    lax.fori_loop(0, n * (nb - 2), inner_column, 0)
    rows = pl.ds(ROWS, ny)
    for face, out in zip(faces, (bx_a, bx_b)):
        for k, lanes in lane_chunks(nz):
            copies.start("out", acc.at[pl.ds(face + RIM, RIM), k, rows, :], out.at[:, :, lanes])
    copies.finish()


def interior_y_kernel(acc_in, field, u, after, acc, token, es, us, ws, vs, hs):
    _, nx, ny, nz = u.shape
    n, nb = nz // LANES, ny // ROWS

    def rows(x, carry):
        y_plane(field, u, acc, (es, us, ws, vs, hs), x, n, ((1, nb - 1),))
        return carry

    lax.fori_loop(RIM, nx - RIM, rows, 0)
    token[...] = jnp.zeros_like(token)


def interior_x_kernel(acc_in, field, u, acc):
    _, nx, ny, nz = u.shape
    n, nb = nz // LANES, ny // ROWS

    def column(i, carry):
        x_column(field, u, acc, lax.rem(i, n), 1 + lax.div(i, n), ((RIM, nx - RIM),))
        return carry

    lax.fori_loop(0, n * (nb - 2), column, 0)


ANY = pl.BlockSpec(memory_space=pl.ANY)
INSIDE = pl.BlockSpec(memory_space=pltpu.VMEM)


def stream_scratch(nx, ny, nz):
    return [pltpu.VMEM((nz // LANES, ny + 3 * ROWS, LANES), jnp.float32)] * 5


def shapes(*dims):
    return jax.ShapeDtypeStruct(dims, jnp.float32)


def edge_rows(shape, field, acc, u, xa, xb, ya, yb):
    nx, ny, nz = shape
    return pl.pallas_call(
        edge_rows_kernel,
        in_specs=[INSIDE] * 3 + [ANY] * 4,
        out_specs=[INSIDE] * 2 + [ANY] * 2,
        out_shape=[rimmed(shape)] * 2 + [shapes(*side_shape(shape))] * 2,
        input_output_aliases={0: 0, 1: 1},
        scratch_shapes=stream_scratch(nx, ny, nz)
        + [pltpu.VMEM(side_shape(shape), jnp.float32)] * 4
        + [pltpu.SemaphoreType.DMA((24,))],
        name="edge_rows",
        cost_estimate=estimate(shapes(*shape), 30),
        compiler_params=pltpu.CompilerParams(vmem_limit_bytes=8 * MIB),
    )(field, acc, u, xa, xb, ya, yb)


def edge_planes(shape, acc, field, u):
    nx, ny, nz = shape
    return pl.pallas_call(
        edge_planes_kernel,
        in_specs=[INSIDE] * 3,
        out_specs=[INSIDE] + [ANY] * 2,
        out_shape=[rimmed(shape)] + [shapes(RIM, ny, nz)] * 2,
        input_output_aliases={0: 0},
        scratch_shapes=stream_scratch(nx, ny, nz) + [pltpu.SemaphoreType.DMA((8,))],
        name="edge_planes",
        cost_estimate=estimate(shapes(*shape), 20),
        compiler_params=pltpu.CompilerParams(vmem_limit_bytes=4 * MIB),
    )(acc, field, u)


def interior_y(shape, acc, field, u, after):
    return pl.pallas_call(
        interior_y_kernel,
        in_specs=[INSIDE] * 3 + [ANY],
        out_specs=[INSIDE] * 2,
        out_shape=[rimmed(shape), shapes(ROWS, LANES)],
        input_output_aliases={0: 0},
        scratch_shapes=stream_scratch(*shape),
        name="interior_y",
        cost_estimate=estimate(shapes(*shape), 30),
        compiler_params=pltpu.CompilerParams(vmem_limit_bytes=4 * MIB),
    )(acc, field, u, after)


def interior_x(shape, acc, field, u):
    return pl.pallas_call(
        interior_x_kernel,
        in_specs=[INSIDE] * 3,
        out_specs=INSIDE,
        out_shape=rimmed(shape),
        input_output_aliases={0: 0},
        name="interior_x",
        cost_estimate=estimate(shapes(*shape), 30),
        compiler_params=pltpu.CompilerParams(vmem_limit_bytes=4 * MIB),
    )(acc, field, u)


def corner_kernel(ya, yb, token, ca, cb):
    n, rows, _ = ya.shape
    faces, _ = face_starts(rows // RIM)
    for k in range(n):
        for out, face in ((ca, faces[0]), (cb, faces[1])):
            for i in range(RIM):
                row = pl.ds(RIM * (face + i), RIM)
                out[k, pl.ds(RIM * i, RIM), :] = ya[k, row, :]
                out[k, pl.ds(SECOND + RIM * i, RIM), :] = yb[k, row, :]


def corner_faces(ya, yb, token):
    return pl.pallas_call(
        corner_kernel,
        in_specs=[INSIDE] * 3,
        out_specs=[INSIDE] * 2,
        out_shape=[shapes(ya.shape[0], 3 * ROWS, LANES)] * 2,
        name="corner_faces",
        compiler_params=pltpu.CompilerParams(vmem_limit_bytes=4 * MIB),
    )(ya, yb, token)


def sweeps_kernel(f0_in, xa, xb, ya, yb, ca, cb, route_ref, perm_ref, zmean_ref, f0, out_hbm, *rest):
    slot_refs, (f1, step, sgn, sem) = rest[:-4], rest[-4:]
    nx, ny, nz = out_hbm.shape
    n = nz // LANES
    nb = ny // ROWS
    copies = Copies(sem)
    _, rims = face_starts(nx)
    upper = first_is_above("narrow")
    parts = pieces(nx)
    for block, rim in ((xa, rims[0]), (xb, rims[1])):
        for k, lanes in lane_chunks(nz):
            copies.start("rim", block.at[:, :, lanes], f0.at[pl.ds(rim, RIM), k, pl.ds(ROWS, ny), :])
    place_rows(f0, RIM, nx, upper, ya, yb, ny)
    place_rows(f0, rims[0], RIM, upper, ca, ca, ny, SECOND)
    place_rows(f0, rims[1], RIM, upper, cb, cb, ny, SECOND)
    copies.wait("rim")

    def sweep(src, dst, x_first, x_end, y_first, blocks, mode):
        def plane(x, carry):
            for b in range(blocks):
                y = ROWS + y_first + b * ROWS
                ys = pl.ds(y, ROWS)
                f = [src[x, k, ys, :] for k in range(n)]
                fp = rolled(f, 1, lambda k: f[k])
                fm = rolled(f, -1, lambda k: f[k])
                for k in range(n):
                    if mode == "first":
                        st = (PSEUDO_STEP * f[k]) * lax.rsqrt(f[k] * f[k] + 1.0)
                        sg = jnp.where(f[k] > 0, 1.0, -1.0)
                        step[x, k, ys, :] = st
                        sgn[x, k, ys, :] = sg
                    else:
                        st = step[x, k, ys, :]
                        sg = sgn[x, k, ys, :]
                    p = sg * f[k]

                    def term(lo, hi):
                        m = jnp.maximum(p - jnp.minimum(sg * lo, sg * hi), 0.0)
                        return m * m

                    sq = term(src[x - 1, k, ys, :], src[x + 1, k, ys, :])
                    sq = sq + term(src[x, k, pl.ds(y - 1, ROWS), :], src[x, k, pl.ds(y + 1, ROWS), :])
                    sq = sq + term(fm[k], fp[k])
                    root = sq * lax.rsqrt(jnp.maximum(sq, 1e-30))
                    new = f[k] - st * (root - 1.0)
                    dst[x, k, ys, :] = new
                    if mode == "last":
                        sgn[x, k, ys, :] = new * lax.rsqrt(new * new + 1.0)
            return carry

        lax.fori_loop(x_first, x_end, plane, 0)

    sweep(f0, f1, 1, nx + 5, -2, nb + 1, "first")
    sweep(f1, f0, 2, nx + 4, -1, nb + 1, "middle")
    for x0, count in parts:
        sweep(f0, f1, RIM + x0, RIM + x0 + count, 0, nb, "last")
        for k, lanes in lane_chunks(nz):
            copies.start("out", f1.at[pl.ds(RIM + x0, count), k, pl.ds(ROWS, ny), :], out_hbm.at[pl.ds(x0, count), :, lanes])

    half = TILE // 2
    tz = nz // TILE
    blocks = [(tx, ty) for tx in range(nx // TILE) for ty in range(ny // TILE)]

    def two(a):
        high = a.astype(jnp.bfloat16)
        return high, (a - high.astype(jnp.float32)).astype(jnp.bfloat16)

    summed = []
    for tx, ty in blocks:
        for cx in range(half):
            row = []
            for k in range(n):
                x, y = RIM + tx * TILE + 2 * cx, ROWS + ty * TILE
                even, odd = pl.ds(y, half, 2), pl.ds(y + 1, half, 2)
                row.append((sgn[x, k, even, :] + sgn[x, k, odd, :]) + (sgn[x + 1, k, even, :] + sgn[x + 1, k, odd, :]))
            summed.append(jnp.concatenate(row, axis=1))
    summed = jnp.concatenate(summed, axis=0)
    zm = zmean_ref[...]
    dims = (((1,), (1,)), ((), ()))
    high, low = two(summed)
    mean = lax.dot_general(zm, high, dims, preferred_element_type=jnp.float32)
    mean = mean + lax.dot_general(zm, low, dims, preferred_element_type=jnp.float32)
    area = half * half
    tiles = jnp.concatenate(
        [
            jnp.concatenate([mean[c * tz : (c + 1) * tz, i * area : (i + 1) * area] for c in range(half)], axis=1)
            for i in range(len(blocks))
        ],
        axis=0,
    )
    pm = perm_ref[...]
    high, low = two(tiles)
    tiles = 0.5 - (jnp.dot(high, pm, preferred_element_type=jnp.float32) + jnp.dot(low, pm, preferred_element_type=jnp.float32))
    owners = len(slot_refs)
    capacity = slot_refs[0].shape[0]
    count = len(blocks) * tz
    route = route_ref[...] - lax.axis_index("wide")
    route = jnp.where(route < 0, route + owners, route)
    padded = -(-owners // ROWS) * ROWS
    matches = lax.broadcasted_iota(jnp.int32, (padded, count), 0) == route
    ordered = lax.broadcasted_iota(jnp.int32, (count, count), 0) < lax.broadcasted_iota(jnp.int32, (count, count), 1)
    match = jnp.where(matches, 1.0, 0.0)
    earlier = jnp.dot(
        match.astype(jnp.bfloat16), jnp.where(ordered, 1.0, 0.0).astype(jnp.bfloat16), preferred_element_type=jnp.float32
    )
    position = jnp.sum(earlier * match, axis=0, keepdims=True).astype(jnp.int32)
    target = route * capacity + position
    slots = lax.broadcasted_iota(jnp.int32, (owners * capacity, count), 0)
    pick = jnp.where(slots == target, 1.0, 0.0).astype(jnp.bfloat16)
    high, low = two(tiles)
    packed = jnp.dot(pick, high, preferred_element_type=jnp.float32) + jnp.dot(pick, low, preferred_element_type=jnp.float32)
    for i, ref in enumerate(slot_refs):
        ref[...] = packed[i * capacity : (i + 1) * capacity, :]
    copies.finish()


def sweeps(shape, moved, rims, route, owners, capacity):
    nx, ny, nz = shape
    half = TILE // 2
    tz = nz // TILE
    r = np.arange(half * tz)
    z = np.arange(nz)
    zmean = ((z[None, :] // TILE == (r % tz)[:, None]) & ((z[None, :] % TILE) // 2 == (r // tz)[:, None])) / 16.0
    src = np.arange(half**3)
    perm = np.zeros((half**3, half**3))
    perm[src, (src % half**2) * half + src // half**2] = 1.0
    return pl.pallas_call(
        sweeps_kernel,
        in_specs=[INSIDE] + [ANY] * 2 + [INSIDE] * 7,
        out_specs=[INSIDE, ANY] + [INSIDE] * owners,
        out_shape=[rimmed(shape), shapes(nx, ny, nz)] + [shapes(capacity, half**3)] * owners,
        input_output_aliases={0: 0},
        scratch_shapes=[rimmed(shape)] * 3 + [pltpu.SemaphoreType.DMA((64,))],
        name="sweeps",
        cost_estimate=estimate(shapes(*shape), 100),
        compiler_params=pltpu.CompilerParams(vmem_limit_bytes=30 * MIB),
    )(moved, *rims, route, jnp.asarray(perm, jnp.bfloat16), jnp.asarray(zmean, jnp.bfloat16))


def faces_kernel(core, xa_hbm, xb_hbm, ya_hbm, yb_hbm, x, rows, y, sem):
    nx, ny, nz = core.shape
    copies = Copies(sem)
    faces, _ = face_starts(nx)
    upper = first_is_above("narrow")
    groups = pieces(nx)
    copies.start("xa", core.at[pl.ds(faces[0], RIM)], x.at[0])
    copies.start("xb", core.at[pl.ds(faces[1], RIM)], x.at[1])
    for x0, count in groups:
        xs = pl.ds(x0, count)
        copies.start(x0, core.at[xs, pl.ds(0, ROWS), :], rows.at[0, xs])
        copies.start(x0, core.at[xs, pl.ds(ny - ROWS, ROWS), :], rows.at[1, xs])
    copies.wait("xa")
    copies.start("out", x.at[0], xa_hbm)
    copies.wait("xb")
    copies.start("out", x.at[1], xb_hbm)

    def plane(i, carry):
        for k, lanes in lane_chunks(nz):
            lo, hi = rows[0, i, pl.ds(0, RIM), lanes], rows[1, i, pl.ds(ROWS - RIM, RIM), lanes]
            y[0, k, pl.ds(RIM * i, RIM), :] = jnp.where(upper, hi, lo)
            y[1, k, pl.ds(RIM * i, RIM), :] = jnp.where(upper, lo, hi)
        return carry

    for x0, count in groups:
        side = pl.ds(RIM * x0, RIM * count)
        copies.wait(x0)
        lax.fori_loop(x0, x0 + count, plane, 0)
        copies.start("out", y.at[0, :, side], ya_hbm.at[:, side])
        copies.start("out", y.at[1, :, side], yb_hbm.at[:, side])
    copies.finish()


def own_faces(block):
    nx, ny, nz = block.shape
    f32 = jnp.float32
    return pl.pallas_call(
        faces_kernel,
        in_specs=[ANY],
        out_specs=[ANY] * 4,
        out_shape=[shapes(RIM, ny, nz)] * 2 + [shapes(*side_shape(block.shape))] * 2,
        scratch_shapes=[
            pltpu.VMEM((2, RIM, ny, nz), f32),
            pltpu.VMEM((2, nx, ROWS, nz), f32),
            pltpu.VMEM((2,) + side_shape(block.shape), f32),
            pltpu.SemaphoreType.DMA((24,)),
        ],
        name="own_faces",
        compiler_params=pltpu.CompilerParams(vmem_limit_bytes=61 * MIB),
    )(block)


def gather_kernel(*refs):
    blocks, out, sem = refs[:-2], refs[-2], refs[-1]
    me, owners = lax.axis_index("wide"), len(blocks)
    copies = [
        pltpu.make_async_copy(b, out.at[lax.rem(me - i + owners, owners)], sem.at[i]) for i, b in enumerate(blocks)
    ]
    for c in copies:
        c.start()
    for c in copies:
        c.wait()


def gather_blocks(blocks):
    return pl.pallas_call(
        gather_kernel,
        in_specs=[INSIDE] * len(blocks),
        out_specs=ANY,
        out_shape=shapes(len(blocks), *blocks[0].shape),
        scratch_shapes=[pltpu.SemaphoreType.DMA((len(blocks),))],
        name="gather_blocks",
        compiler_params=pltpu.CompilerParams(vmem_limit_bytes=8 * MIB),
    )(*blocks)


def trade(axis, first, second):
    peers = lax.axis_size(axis)
    return (
        lax.ppermute(first, axis, [(i, i ^ 1) for i in range(peers)]),
        lax.ppermute(second, axis, [(i, (i + 1 if i % 2 else i - 1) % peers) for i in range(peers)]),
    )


def on_device(level_set, velocity, box_owner):
    owners = lax.axis_size("wide")
    xa, xb, ya, yb = own_faces(level_set)
    xa, xb = trade("wide", xa, xb)
    ya, yb = trade("narrow", ya, yb)
    field, acc, u = along_z(level_set, velocity)
    shape = level_set.shape
    field, acc, yf_a, yf_b = edge_rows(shape, field, acc, u, xa, xb, ya, yb)
    ya, yb = trade("narrow", yf_a, yf_b)
    acc, bx_a, bx_b = edge_planes(shape, acc, field, u)
    xa, xb = trade("wide", bx_a, bx_b)
    acc, token = interior_y(shape, acc, field, u, bx_a)
    ca, cb = trade("wide", *corner_faces(ya, yb, token))
    moved = interior_x(shape, acc, field, u)
    tile_count = box_owner.shape[2]
    capacity = max(2, 5 * tile_count // (2 * owners))
    route = box_owner.reshape(1, tile_count)
    _, surface, *slots = sweeps(shape, moved, (xa, xb, ya, yb, ca, cb), route, owners, capacity)
    received = [slots[0]]
    for step in range(1, owners):
        received.append(lax.ppermute(slots[step], "wide", [(i, (i + step) % owners) for i in range(owners)]))
    box_slots = gather_blocks(received)
    return (surface, box_slots.reshape(1, 1, owners * capacity, -1))


def solution(mesh):
    return jax.shard_map(
        on_device,
        mesh=mesh,
        in_specs=(
            P("wide", "narrow", None),
            P(None, "wide", "narrow", None),
            P("wide", "narrow", None, None),
        ),
        out_specs=(P("wide", "narrow", None), P("wide", "narrow", None, None)),
        check_vma=False,
    )
```

profile of v0, /device:TPU:11, one launch (start us, length us, event | category | flops | bytes accessed | tf_op | source)
XLA Modules:
  0.0 111.3 jit_solution(18117896251324663410)
XLA Ops:
  0.6 2.3 %own_faces.1 = (f32[3,64,512]{2,1,0:T(8,128)}, f32[3,64,512]{2,1,0:T(8,128)}, f32[4,96,128]{2,1,0:T(8,128)}, f32[4,96,128]{2,1,0:T(8,128)}) custom-call(f32[32,64,512]{2,1,0:T(8,128)} %core.3), custom_call_target="tpu_custom_call" | custom-call | tf_op jit(solution)/shard_map/own_faces/pallas_call | solution.py:617
  3.0 0.7 collective-permute-start
  3.7 1.3 %collective-permute-start.1 = (f32[3,64,512]{2,1,0:T(8,128)}, f32[3,64,512]{2,1,0:T(8,128)S(1)}, u32[]{:S(2)}, u32[]{:S(2)}) collective-permute-start(f32[3,64,512]{2,1,0:T(8,128)} %get-tuple-element.33), channel_id=1, source_target_pairs={{0,7},{1,2},{2,1},{3,4},{4,3},{5,6},{6,5},{7,0},{8,15},{9,10},{10,... | collective-permute-start | bytes 1179656 | tf_op jit(solution)/shard_map/ppermute | solution.py:661
  5.0 0.3 collective-permute-start.2
  5.2 2.2 %collective-permute-start.3 = (f32[4,96,128]{2,1,0:T(8,128)}, f32[4,96,128]{2,1,0:T(8,128)S(1)}, u32[]{:S(2)}, u32[]{:S(2)}) collective-permute-start(f32[4,96,128]{2,1,0:T(8,128)} %get-tuple-element.35), channel_id=1, source_target_pairs={{0,24},{8,16},{16,8},{24,0},{1,25},{9,17},{17,9},{25,1},{2,26},{10... | collective-permute-start | bytes 589832 | tf_op jit(solution)/shard_map/ppermute | solution.py:661
  7.4 18.0 %along_z.1 = (f32[38,4,80,128]{3,2,1,0:T(8,128)S(1)}, f32[38,4,80,128]{3,2,1,0:T(8,128)S(1)}, bf16[2,32,64,512]{3,2,1,0:T(8,128)(2,1)S(1)}) custom-call(f32[32,64,512]{2,1,0:T(8,128)} %core.3, bf16[3,32,64,512]{3,2,1,0:T(8,128)(2,1)} %u_hbm.1), custom_call_target="tpu_custom_call" | custom-call | flops 62914560 | bytes 8388608 | tf_op jit(solution)/shard_map/along_z/pallas_call | solution.py:116
  25.4 0.0 collective-permute-done.2.ya_hbm
  25.4 0.0 collective-permute-done.3.yb_hbm
  25.4 0.0 collective-permute-done.xa
  25.4 0.0 collective-permute-done.1.xb
  25.4 7.0 %edge_rows.1 = (f32[38,4,80,128]{3,2,1,0:T(8,128)S(1)}, f32[38,4,80,128]{3,2,1,0:T(8,128)S(1)}, f32[4,96,128]{2,1,0:T(8,128)S(1)}, f32[4,96,128]{2,1,0:T(8,128)S(1)}) custom-call(f32[38,4,80,128]{3,2,1,0:T(8,128)S(1)} %get-tuple-element.29.field_in, f32[38,4,80,128]{3,2,1,0:T(8,128)S(1)} %get-tuple-element.30.acc_in, ...), custom_call_target="tpu_custom_call", output_to_operand_aliasing={{0}: (0, {}), {1}: (1, {})} | custom-call | flops 31457280 | bytes 8388608 | tf_op jit(solution)/shard_map/edge_rows/pallas_call | solution.py:363
  32.4 3.1 %edge_planes.1 = (f32[38,4,80,128]{3,2,1,0:T(8,128)S(1)}, f32[3,64,512]{2,1,0:T(8,128)S(1)}, f32[3,64,512]{2,1,0:T(8,128)S(1)}) custom-call(f32[38,4,80,128]{3,2,1,0:T(8,128)S(1)} %get-tuple-element.36.acc_in, f32[38,4,80,128]{3,2,1,0:T(8,128)S(1)} %get-tuple-element.37.field, ...), custom_call_target="tpu_custom_call", output_to_operand_aliasing={{0}: (0, {})} | custom-call | flops 20971520 | bytes 8388608 | tf_op jit(solution)/shard_map/edge_planes/pallas_call | solution.py:380
  35.5 1.1 collective-permute-start.5
  36.6 0.0 collective-permute-start.4
  36.6 0.3 collective-permute-start.6
  36.9 1.2 %collective-permute-start.7 = (f32[4,96,128]{2,1,0:T(8,128)S(1)}, f32[4,96,128]{2,1,0:T(8,128)S(1)}, u32[]{:S(2)}, u32[]{:S(2)}) collective-permute-start(f32[4,96,128]{2,1,0:T(8,128)S(1)} %get-tuple-element.43), channel_id=1, source_target_pairs={{0,24},{8,16},{16,8},{24,0},{1,25},{9,17},{17,9},{25,1},{2,26},{10... | collective-permute-start | bytes 589832 | tf_op jit(solution)/shard_map/ppermute | solution.py:661
  38.1 5.6 %interior_y.1 = (f32[38,4,80,128]{3,2,1,0:T(8,128)S(1)}, f32[8,128]{1,0:T(8,128)S(1)}) custom-call(f32[38,4,80,128]{3,2,1,0:T(8,128)S(1)} %get-tuple-element.38.acc_in, f32[38,4,80,128]{3,2,1,0:T(8,128)S(1)} %get-tuple-element.37.field, bf16[2,32,64,512]{3,2,1,0:T(8,128)(2,1)S(1)} %get-tuple-element.31.u, ...), custom_call_target="tpu_custom_call", output_to_operand_aliasing={{0}: (0, {})} | custom-call | flops 31457280 | bytes 8388608 | tf_op jit(solution)/shard_map/interior_y/pallas_call | solution.py:394
  43.7 0.0 collective-permute-done.6.ya
  43.7 3.0 %collective-permute-done.7.yb = f32[4,96,128]{2,1,0:T(8,128)S(1)} collective-permute-done((f32[4,96,128]{2,1,0:T(8,128)S(1)}, f32[4,96,128]{2,1,0:T(8,128)S(1)}, u32[]{:S(2)}, u32[]{:S(2)}) %collective-permute-start.7) | collective-permute-done | bytes 196640 | tf_op jit(solution)/shard_map/ppermute | solution.py:661
  46.8 1.4 %collective-permute-start.8 = (f32[4,24,128]{2,1,0:T(8,128)S(1)}, f32[4,24,128]{2,1,0:T(8,128)S(1)}, u32[]{:S(2)}, u32[]{:S(2)}) collective-permute-start(f32[4,24,128]{2,1,0:T(8,128)S(1)} %get-tuple-element.45), channel_id=1, source_target_pairs={{0,1},{1,0},{2,3},{3,2},{4,5},{5,4},{6,7},{7,6},{8,9},{9,8},{10,11... | collective-permute-start | bytes 147464 | tf_op jit(solution)/shard_map/ppermute | solution.py:660
  48.2 1.3 %collective-permute-start.9 = (f32[4,24,128]{2,1,0:T(8,128)S(1)}, f32[4,24,128]{2,1,0:T(8,128)S(1)}, u32[]{:S(2)}, u32[]{:S(2)}) collective-permute-start(f32[4,24,128]{2,1,0:T(8,128)S(1)} %get-tuple-element.46), channel_id=1, source_target_pairs={{0,7},{1,2},{2,1},{3,4},{4,3},{5,6},{6,5},{7,0},{8,15},{9,10},{10,... | collective-permute-start | bytes 147464 | tf_op jit(solution)/shard_map/ppermute | solution.py:661
  49.5 0.0 copy-start
  49.5 0.0 copy-start.1
  49.5 0.0 copy-start.2
  49.5 4.5 %interior_x.1.f0_in = f32[38,4,80,128]{3,2,1,0:T(8,128)S(1)} custom-call(f32[38,4,80,128]{3,2,1,0:T(8,128)S(1)} %get-tuple-element.40.acc_in, f32[38,4,80,128]{3,2,1,0:T(8,128)S(1)} %get-tuple-element.37.field, bf16[2,32,64,512]{3,2,1,0:T(8,128)(2,1)S(1)} %get-tuple-element.31.u), custom_call_target="tpu_custom_call", output_to_operand_aliasing={{}: (0, {})} | custom-call | flops 31457280 | bytes 8388608 | tf_op jit(solution)/shard_map/interior_x/pallas_call | solution.py:408
  54.0 0.0 collective-permute-done.8.ca
  54.0 0.0 collective-permute-done.9.cb
  54.0 0.0 collective-permute-done.5.xb
  54.0 0.0 collective-permute-done.4.xa
  54.0 0.0 copy-done
  54.0 0.0 copy-done.1
  54.1 0.0 copy-done.2
  54.1 20.6 %sweeps.1 = (f32[38,4,80,128]{3,2,1,0:T(8,128)S(1)}, f32[32,64,512]{2,1,0:T(8,128)}, f32[80,512]{1,0:T(8,128)S(1)}, f32[80,512]{1,0:T(8,128)S(1)}, f32[80,512]{1...) custom-call(f32[38,4,80,128]{3,2,1,0:T(8,128)S(1)} %interior_x.1.f0_, ...), custom_call_target="tpu_custom_call", output_to_operand_aliasing={{0}: (0, {})} | custom-call | flops 104857600 | bytes 8388608 | tf_op jit(solution)/shard_map/sweeps/pallas_call | solution.py:568
  74.6 0.5 collective-permute-start.10
  75.2 2.7 %collective-permute-start.11 = (f32[80,512]{1,0:T(8,128)S(1)}, f32[80,512]{1,0:T(8,128)S(1)}, u32[]{:S(2)}, u32[]{:S(2)}) collective-permute-start(f32[80,512]{1,0:T(8,128)S(1)} %get-tuple-element.50), channel_id=1, source_target_pairs={{0,2},{1,3},{2,4},{3,5},{4,6},{5,7},{6,0},{7,1},{8,10},{9,11},{10,... | collective-permute-start | bytes 491528 | tf_op jit(solution)/shard_map/ppermute | solution.py:685
  77.8 3.6 %collective-permute-start.12 = (f32[80,512]{1,0:T(8,128)S(1)}, f32[80,512]{1,0:T(8,128)S(1)}, u32[]{:S(2)}, u32[]{:S(2)}) collective-permute-start(f32[80,512]{1,0:T(8,128)S(1)} %get-tuple-element.51), channel_id=1, source_target_pairs={{0,3},{1,4},{2,5},{3,6},{4,7},{5,0},{6,1},{7,2},{8,11},{9,12},{10,... | collective-permute-start | bytes 491528 | tf_op jit(solution)/shard_map/ppermute | solution.py:685
  81.4 0.0 collective-permute-start.13
  81.4 1.7 %collective-permute-start.14 = (f32[80,512]{1,0:T(8,128)S(1)}, f32[80,512]{1,0:T(8,128)S(1)}, u32[]{:S(2)}, u32[]{:S(2)}) collective-permute-start(f32[80,512]{1,0:T(8,128)S(1)} %get-tuple-element.53), channel_id=1, source_target_pairs={{0,5},{1,6},{2,7},{3,0},{4,1},{5,2},{6,3},{7,4},{8,13},{9,14},{10,... | collective-permute-start | bytes 491528 | tf_op jit(solution)/shard_map/ppermute | solution.py:685
  83.1 0.0 collective-permute-done.10.refs_1_
  83.1 2.4 %collective-permute-start.15 = (f32[80,512]{1,0:T(8,128)S(1)}, f32[80,512]{1,0:T(8,128)S(1)}, u32[]{:S(2)}, u32[]{:S(2)}) collective-permute-start(f32[80,512]{1,0:T(8,128)S(1)} %get-tuple-element.54), channel_id=1, source_target_pairs={{0,6},{1,7},{2,0},{3,1},{4,2},{5,3},{6,4},{7,5},{8,14},{9,15},{10,... | collective-permute-start | bytes 491528 | tf_op jit(solution)/shard_map/ppermute | solution.py:685
  85.5 0.0 collective-permute-done.11.refs_2_
  85.5 1.7 %collective-permute-start.16 = (f32[80,512]{1,0:T(8,128)S(1)}, f32[80,512]{1,0:T(8,128)S(1)}, u32[]{:S(2)}, u32[]{:S(2)}) collective-permute-start(f32[80,512]{1,0:T(8,128)S(1)} %get-tuple-element.55), channel_id=1, source_target_pairs={{0,7},{1,0},{2,1},{3,2},{4,3},{5,4},{6,5},{7,6},{8,15},{9,8},{10,9... | collective-permute-start | bytes 491528 | tf_op jit(solution)/shard_map/ppermute | solution.py:685
  87.2 0.1 collective-permute-done.12.refs_3_
  87.3 15.2 %collective-permute-done.13.refs_4_ = f32[80,512]{1,0:T(8,128)S(1)} collective-permute-done((f32[80,512]{1,0:T(8,128)S(1)}, f32[80,512]{1,0:T(8,128)S(1)}, u32[]{:S(2)}, u32[]{:S(2)}) %collective-permute-start.13) | collective-permute-done | bytes 163872 | tf_op jit(solution)/shard_map/ppermute | solution.py:685
  102.5 0.0 collective-permute-done.14.refs_5_
  102.5 7.6 %collective-permute-done.15.refs_6_ = f32[80,512]{1,0:T(8,128)S(1)} collective-permute-done((f32[80,512]{1,0:T(8,128)S(1)}, f32[80,512]{1,0:T(8,128)S(1)}, u32[]{:S(2)}, u32[]{:S(2)}) %collective-permute-start.15) | collective-permute-done | bytes 163872 | tf_op jit(solution)/shard_map/ppermute | solution.py:685
  110.1 0.1 collective-permute-done.16.refs_7_
  110.2 1.1 gather_blocks.1
  (1 shorter events, 0.0 us)
Async XLA Ops:
  3.0 22.4 %collective-permute-start = (f32[3,64,512]{2,1,0:T(8,128)}, f32[3,64,512]{2,1,0:T(8,128)S(1)}, u32[]{:S(2)}, u32[]{:S(2)}) collective-permute-start(f32[3,64,512]{2,1,0:T(8,128)} %get-tuple-element.32), channel_id=1, source_target_pairs={{0,1},{1,0},{2,3},{3,2},{4,5},{5,4},{6,7},{7,6},{8,9},{9,8},{10,11... | collective-permute-start | bytes 1179656 | tf_op jit(solution)/shard_map/ppermute | solution.py:660
  3.7 21.7 %collective-permute-start.1 = (f32[3,64,512]{2,1,0:T(8,128)}, f32[3,64,512]{2,1,0:T(8,128)S(1)}, u32[]{:S(2)}, u32[]{:S(2)}) collective-permute-start(f32[3,64,512]{2,1,0:T(8,128)} %get-tuple-element.33), channel_id=1, source_target_pairs={{0,7},{1,2},{2,1},{3,4},{4,3},{5,6},{6,5},{7,0},{8,15},{9,10},{10,... | collective-permute-start | bytes 1179656 | tf_op jit(solution)/shard_map/ppermute | solution.py:661
  5.0 20.4 %collective-permute-start.2 = (f32[4,96,128]{2,1,0:T(8,128)}, f32[4,96,128]{2,1,0:T(8,128)S(1)}, u32[]{:S(2)}, u32[]{:S(2)}) collective-permute-start(f32[4,96,128]{2,1,0:T(8,128)} %get-tuple-element.34), channel_id=1, source_target_pairs={{0,8},{8,0},{16,24},{24,16},{1,9},{9,1},{17,25},{25,17},{2,10},{10... | collective-permute-start | bytes 589832 | tf_op jit(solution)/shard_map/ppermute | solution.py:660
  5.2 20.2 %collective-permute-start.3 = (f32[4,96,128]{2,1,0:T(8,128)}, f32[4,96,128]{2,1,0:T(8,128)S(1)}, u32[]{:S(2)}, u32[]{:S(2)}) collective-permute-start(f32[4,96,128]{2,1,0:T(8,128)} %get-tuple-element.35), channel_id=1, source_target_pairs={{0,24},{8,16},{16,8},{24,0},{1,25},{9,17},{17,9},{25,1},{2,26},{10... | collective-permute-start | bytes 589832 | tf_op jit(solution)/shard_map/ppermute | solution.py:661
  35.5 18.5 %collective-permute-start.5 = (f32[3,64,512]{2,1,0:T(8,128)S(1)}, f32[3,64,512]{2,1,0:T(8,128)S(1)}, u32[]{:S(2)}, u32[]{:S(2)}) collective-permute-start(f32[3,64,512]{2,1,0:T(8,128)S(1)} %get-tuple-element.41), channel_id=1, source_target_pairs={{0,7},{1,2},{2,1},{3,4},{4,3},{5,6},{6,5},{7,0},{8,15},{9,10},{10,... | collective-permute-start | bytes 1179656 | tf_op jit(solution)/shard_map/ppermute | solution.py:661
  36.6 17.4 %collective-permute-start.4 = (f32[3,64,512]{2,1,0:T(8,128)S(1)}, f32[3,64,512]{2,1,0:T(8,128)S(1)}, u32[]{:S(2)}, u32[]{:S(2)}) collective-permute-start(f32[3,64,512]{2,1,0:T(8,128)S(1)} %get-tuple-element.39.after), channel_id=1, source_target_pairs={{0,1},{1,0},{2,3},{3,2},{4,5},{5,4},{6,7},{7,6},{8,9},{9,8},{10,11... | collective-permute-start | bytes 1179656 | tf_op jit(solution)/shard_map/ppermute | solution.py:660
  36.6 7.1 %collective-permute-start.6 = (f32[4,96,128]{2,1,0:T(8,128)S(1)}, f32[4,96,128]{2,1,0:T(8,128)S(1)}, u32[]{:S(2)}, u32[]{:S(2)}) collective-permute-start(f32[4,96,128]{2,1,0:T(8,128)S(1)} %get-tuple-element.42), channel_id=1, source_target_pairs={{0,8},{8,0},{16,24},{24,16},{1,9},{9,1},{17,25},{25,17},{2,10},{10... | collective-permute-start | bytes 589832 | tf_op jit(solution)/shard_map/ppermute | solution.py:660
  36.9 9.9 %collective-permute-start.7 = (f32[4,96,128]{2,1,0:T(8,128)S(1)}, f32[4,96,128]{2,1,0:T(8,128)S(1)}, u32[]{:S(2)}, u32[]{:S(2)}) collective-permute-start(f32[4,96,128]{2,1,0:T(8,128)S(1)} %get-tuple-element.43), channel_id=1, source_target_pairs={{0,24},{8,16},{16,8},{24,0},{1,25},{9,17},{17,9},{25,1},{2,26},{10... | collective-permute-start | bytes 589832 | tf_op jit(solution)/shard_map/ppermute | solution.py:661
  46.8 7.2 %collective-permute-start.8 = (f32[4,24,128]{2,1,0:T(8,128)S(1)}, f32[4,24,128]{2,1,0:T(8,128)S(1)}, u32[]{:S(2)}, u32[]{:S(2)}) collective-permute-start(f32[4,24,128]{2,1,0:T(8,128)S(1)} %get-tuple-element.45), channel_id=1, source_target_pairs={{0,1},{1,0},{2,3},{3,2},{4,5},{5,4},{6,7},{7,6},{8,9},{9,8},{10,11... | collective-permute-start | bytes 147464 | tf_op jit(solution)/shard_map/ppermute | solution.py:660
  48.2 5.8 %collective-permute-start.9 = (f32[4,24,128]{2,1,0:T(8,128)S(1)}, f32[4,24,128]{2,1,0:T(8,128)S(1)}, u32[]{:S(2)}, u32[]{:S(2)}) collective-permute-start(f32[4,24,128]{2,1,0:T(8,128)S(1)} %get-tuple-element.46), channel_id=1, source_target_pairs={{0,7},{1,2},{2,1},{3,4},{4,3},{5,6},{6,5},{7,0},{8,15},{9,10},{10,... | collective-permute-start | bytes 147464 | tf_op jit(solution)/shard_map/ppermute | solution.py:661
  49.5 4.6 %copy-start = (bf16[512,512]{1,0:T(8,128)(2,1)S(1)}, bf16[512,512]{1,0:T(8,128)(2,1)}, u32[]{:S(2)}) copy-start(bf16[512,512]{1,0:T(8,128)(2,1)} %constant.4.clone.perm_ref) | copy-start | bytes 1572868
  49.5 4.6 %copy-start.1 = (bf16[256,512]{1,0:T(8,128)(2,1)S(1)}, bf16[256,512]{1,0:T(8,128)(2,1)}, u32[]{:S(2)}) copy-start(bf16[256,512]{1,0:T(8,128)(2,1)} %constant.5.clone.zmean_ref) | copy-start | bytes 786436
  49.5 4.6 %copy-start.2 = (s32[1,1,256,1]{2,3,1,0:T(1,128)S(1)}, s32[1,1,256,1]{2,3,1,0:T(1,128)}, u32[]{:S(2)}) copy-start(s32[1,1,256,1]{2,3,1,0:T(1,128)} %param.7) | copy-start | bytes 3076
  74.6 8.5 %collective-permute-start.10 = (f32[80,512]{1,0:T(8,128)S(1)}, f32[80,512]{1,0:T(8,128)S(1)}, u32[]{:S(2)}, u32[]{:S(2)}) collective-permute-start(f32[80,512]{1,0:T(8,128)S(1)} %get-tuple-element.49), channel_id=1, source_target_pairs={{0,1},{1,2},{2,3},{3,4},{4,5},{5,6},{6,7},{7,0},{8,9},{9,10},{10,1... | collective-permute-start | bytes 491528 | tf_op jit(solution)/shard_map/ppermute | solution.py:685
  75.2 10.3 %collective-permute-start.11 = (f32[80,512]{1,0:T(8,128)S(1)}, f32[80,512]{1,0:T(8,128)S(1)}, u32[]{:S(2)}, u32[]{:S(2)}) collective-permute-start(f32[80,512]{1,0:T(8,128)S(1)} %get-tuple-element.50), channel_id=1, source_target_pairs={{0,2},{1,3},{2,4},{3,5},{4,6},{5,7},{6,0},{7,1},{8,10},{9,11},{10,... | collective-permute-start | bytes 491528 | tf_op jit(solution)/shard_map/ppermute | solution.py:685
  77.8 9.5 %collective-permute-start.12 = (f32[80,512]{1,0:T(8,128)S(1)}, f32[80,512]{1,0:T(8,128)S(1)}, u32[]{:S(2)}, u32[]{:S(2)}) collective-permute-start(f32[80,512]{1,0:T(8,128)S(1)} %get-tuple-element.51), channel_id=1, source_target_pairs={{0,3},{1,4},{2,5},{3,6},{4,7},{5,0},{6,1},{7,2},{8,11},{9,12},{10,... | collective-permute-start | bytes 491528 | tf_op jit(solution)/shard_map/ppermute | solution.py:685
  81.4 21.1 %collective-permute-start.13 = (f32[80,512]{1,0:T(8,128)S(1)}, f32[80,512]{1,0:T(8,128)S(1)}, u32[]{:S(2)}, u32[]{:S(2)}) collective-permute-start(f32[80,512]{1,0:T(8,128)S(1)} %get-tuple-element.52), channel_id=1, source_target_pairs={{0,4},{1,5},{2,6},{3,7},{4,0},{5,1},{6,2},{7,3},{8,12},{9,13},{10,... | collective-permute-start | bytes 491528 | tf_op jit(solution)/shard_map/ppermute | solution.py:685
  81.4 21.1 %collective-permute-start.14 = (f32[80,512]{1,0:T(8,128)S(1)}, f32[80,512]{1,0:T(8,128)S(1)}, u32[]{:S(2)}, u32[]{:S(2)}) collective-permute-start(f32[80,512]{1,0:T(8,128)S(1)} %get-tuple-element.53), channel_id=1, source_target_pairs={{0,5},{1,6},{2,7},{3,0},{4,1},{5,2},{6,3},{7,4},{8,13},{9,14},{10,... | collective-permute-start | bytes 491528 | tf_op jit(solution)/shard_map/ppermute | solution.py:685
  83.1 27.0 %collective-permute-start.15 = (f32[80,512]{1,0:T(8,128)S(1)}, f32[80,512]{1,0:T(8,128)S(1)}, u32[]{:S(2)}, u32[]{:S(2)}) collective-permute-start(f32[80,512]{1,0:T(8,128)S(1)} %get-tuple-element.54), channel_id=1, source_target_pairs={{0,6},{1,7},{2,0},{3,1},{4,2},{5,3},{6,4},{7,5},{8,14},{9,15},{10,... | collective-permute-start | bytes 491528 | tf_op jit(solution)/shard_map/ppermute | solution.py:685
  85.5 24.7 %collective-permute-start.16 = (f32[80,512]{1,0:T(8,128)S(1)}, f32[80,512]{1,0:T(8,128)S(1)}, u32[]{:S(2)}, u32[]{:S(2)}) collective-permute-start(f32[80,512]{1,0:T(8,128)S(1)} %get-tuple-element.55), channel_id=1, source_target_pairs={{0,7},{1,0},{2,1},{3,2},{4,3},{5,4},{6,5},{7,6},{8,15},{9,8},{10,9... | collective-permute-start | bytes 491528 | tf_op jit(solution)/shard_map/ppermute | solution.py:685
where the time goes:
time: 111 us
  Pallas kernels  62.2 us (56%)
  waiting for transfers between devices  26 us (23%)
  starting transfers between devices  22.2 us (20%)
    ppermute x7, waiting for transfers between devices, on_device(): lax.ppermute(slots[step], 'wide', [(i, (i + step) % owners) for i in rang...  22.9 us
    pallas_call x1, Pallas kernels, sweeps(): pl.pallas_call(sweeps_kernel, in_specs=[INSIDE] + [ANY] * 2 + [INSIDE] *...  20.6 us
    pallas_call x1, Pallas kernels, along_z(): pl.pallas_call(along_z_kernel, in_specs=[ANY, ANY], out_specs=[INSIDE] *...  18 us
    ppermute x7, starting transfers between devices, on_device(): lax.ppermute(slots[step], 'wide', [(i, (i + step) % owners) for i in rang...  12.6 us
    pallas_call x1, Pallas kernels, edge_rows(): pl.pallas_call(edge_rows_kernel, in_specs=[INSIDE] * 3 + [ANY] * 4, out_s...  7.02 us
    ppermute x5, starting transfers between devices, trade(): lax.ppermute(second, axis, [(i, (i + 1 if i % 2 else i - 1) % peers) for...  6.95 us
    pallas_call x1, Pallas kernels, interior_y(): pl.pallas_call(interior_y_kernel, in_specs=[INSIDE] * 3 + [ANY], out_spec...  5.63 us
    pallas_call x1, Pallas kernels, interior_x(): pl.pallas_call(interior_x_kernel, in_specs=[INSIDE] * 3, out_specs=INSIDE...  4.52 us
  transfers between devices with their start and end apart: 17, of which 5 were waited for; matrix products, arithmetic and copies ran while one was open for 0% of the time, Pallas kernels for 25%

commit v1 on v0

--- a/solution.py
+++ b/solution.py
@@ -51,7 +51,7 @@
     return out
 
 
-def along_z_kernel(core, u_hbm, field, acc, u, uz, sem):
+def along_z_kernel(core, u_hbm, field, acc, u, uz, ft, ut, es, us, ws, vs, hs, sem):
     nx, ny, nz = core.shape
     copies = Copies(sem)
     bounds = [0, nx // 16, nx // 4, nx // 2, 3 * nx // 4, nx]
@@ -62,43 +62,61 @@
             copies.start(x0, core.at[xs, :, lanes], field.at[pl.ds(x0 + RIM, x1 - x0), k, pl.ds(ROWS, ny), :])
         copies.start(x0, u_hbm.at[2, xs], uz.at[xs])
     copies.start("u", u_hbm.at[pl.ds(0, 2)], u)
+    per = LANES // ny
     for x0, x1 in groups:
         copies.wait(x0)
-        lax.fori_loop(x0, x1, functools.partial(z_plane, field, uz, acc, ny, nz), 0)
+        lax.fori_loop(x0 // per, x1 // per, functools.partial(z_planes, field, uz, acc, ft, ut, (es, us, ws, vs, hs), per), 0)
     copies.finish()
 
 
-def z_plane(field, uz, acc, rows, depth, x, carry):
-    n = depth // LANES
-    zero = jnp.zeros((ROWS, LANES), jnp.float32)
-    eps = 0.75 * WENO_EPS
-    for yb in range(rows // ROWS):
-        ys = pl.ds(yb * ROWS, ROWS)
-        yf = pl.ds(yb * ROWS + ROWS, ROWS)
-        f = [field[x + RIM, k, yf, :] for k in range(n)]
-        fp = rolled(f, 1, lambda k: f[k])
-        fm = rolled(f, -1, lambda k: f[k])
-        e = [(fp[k] - f[k]) - (f[k] - fm[k]) for k in range(n)]
-        ep = rolled(e, 1, lambda k: zero)
-        em = rolled(e, -1, lambda k: zero)
-        epp = rolled(e, 2, lambda k: zero)
-        emm = rolled(e, -2, lambda k: zero)
-        for k in range(n):
-            v = uz[x, ys, pl.ds(k * LANES, LANES)].astype(jnp.float32)
-            up = v > 0
-            c = e[k]
-            a = jnp.where(up, emm[k], epp[k])
-            b = jnp.where(up, em[k], ep[k])
-            d = jnp.where(up, ep[k], em[k])
-            al, be, ga = b - a, c - b, d - c
-            b75, c75 = 0.75 * b, 0.75 * c
-            s1 = (al * al + eps) + b75 * (b + al)
-            s2 = (be * be + eps) + b75 * c
-            s3 = (ga * ga + eps) + c75 * (c - ga)
-            phi = correction(s1, s2, s3, be - al, ga - be)
-            mid = 6.0 * (fp[k] - fm[k]) - (ep[k] - em[k])
-            v12 = v * (1.0 / 12.0)
-            acc[x + RIM, k, yf, :] = f[k] - (v12 * mid - jnp.abs(v12) * phi)
+def z_planes(field, uz, acc, ft, ut, streams, per, i, carry):
+    es, us, ws, vs, hs = streams
+    ny = LANES // per
+    n = field.shape[1]
+    depth = n * LANES
+    rows = pl.ds(ROWS, ny)
+    planes = [per * i + p for p in range(per)]
+    for k in range(n):
+        ft[pl.ds(ROWS + k * LANES, LANES), :] = jnp.concatenate([field[x + RIM, k, rows, :] for x in planes], axis=0).T
+        v = jnp.concatenate([uz[x, :, pl.ds(k * LANES, LANES)] for x in planes], axis=0)
+        ut[pl.ds(k * LANES, LANES), :] = v.astype(jnp.float32).T
+    ft[pl.ds(0, ROWS), :] = jnp.broadcast_to(ft[pl.ds(ROWS, 1), :], (ROWS, LANES))
+    ft[pl.ds(ROWS + depth, ROWS), :] = jnp.broadcast_to(ft[pl.ds(ROWS + depth - 1, 1), :], (ROWS, LANES))
+
+    def at(z):
+        return ft[pl.ds(ROWS + z, ROWS), :]
+
+    blocks = depth // ROWS
+    for b in range(blocks + 1):
+        z = b * ROWS - 2
+        f0 = at(z)
+        es[pl.ds(ROWS + b * ROWS, ROWS), :] = (at(z + 1) - f0) - (f0 - at(z - 1))
+    for b in range(blocks + 1):
+        r = ROWS + b * ROWS
+        e0, e1, e_1 = es[pl.ds(r, ROWS), :], es[pl.ds(r + 1, ROWS), :], es[pl.ds(r - 1, ROWS), :]
+        t = e1 - e0
+        us[pl.ds(r, ROWS), :], ws[pl.ds(r, ROWS), :], vs[pl.ds(r, ROWS), :] = pair_forms(e0, e1, t)
+        hs[pl.ds(r, ROWS), :] = t - (e0 - e_1)
+    for b in range(blocks):
+
+        def of(ref, d):
+            return ref[pl.ds(ROWS + b * ROWS + 2 + d, ROWS), :]
+
+        zs = pl.ds(b * ROWS, ROWS)
+        v = ut[zs, :]
+        up = v > 0
+        s1 = jnp.where(up, of(us, -2), of(vs, 1))
+        s2 = jnp.where(up, of(ws, -1), of(ws, 0))
+        s3 = jnp.where(up, of(vs, 0), of(us, -1))
+        h1 = jnp.where(up, of(hs, -1), of(hs, 1))
+        phi = correction(s1, s2, s3, h1, of(hs, 0))
+        mid = 6.0 * (at(b * ROWS + 1) - at(b * ROWS - 1)) - (of(es, 1) - of(es, -1))
+        v12 = v * (1.0 / 12.0)
+        ut[zs, :] = v12 * mid - jnp.abs(v12) * phi
+    for k in range(n):
+        change = ut[pl.ds(k * LANES, LANES), :].T
+        for p, x in enumerate(planes):
+            acc[x + RIM, k, rows, :] = field[x + RIM, k, rows, :] - change[p * ny : (p + 1) * ny, :]
     return carry
 
 
@@ -118,7 +136,13 @@
         in_specs=[ANY, ANY],
         out_specs=[INSIDE] * 3,
         out_shape=[rimmed(level_set.shape)] * 2 + [in_vmem((2, nx, ny, nz), velocity.dtype)],
-        scratch_shapes=[pltpu.VMEM((nx, ny, nz), velocity.dtype), pltpu.SemaphoreType.DMA((40,))],
+        scratch_shapes=[
+            pltpu.VMEM((nx, ny, nz), velocity.dtype),
+            pltpu.VMEM((nz + 2 * ROWS, LANES), jnp.float32),
+            pltpu.VMEM((nz, LANES), jnp.float32),
+        ]
+        + [pltpu.VMEM((nz + 3 * ROWS, LANES), jnp.float32)] * 5
+        + [pltpu.SemaphoreType.DMA((40,))],
         name="along_z",
         cost_estimate=estimate(level_set, 60),
         compiler_params=pltpu.CompilerParams(vmem_limit_bytes=46 * MIB),

time: 111 us -> 106 us (0.955)
  the two profiles are of different devices: /device:TPU:11 before, /device:TPU:13 now
where the time goes in v1:
time: 106 us
  Pallas kernels  57.1 us (54%)
  waiting for transfers between devices  26 us (25%)
  starting transfers between devices  22.2 us (21%)
    ppermute x7, waiting for transfers between devices, on_device(): lax.ppermute(slots[step], 'wide', [(i, (i + step) % owners) for i in rang...  22.9 us
    pallas_call x1, Pallas kernels, sweeps(): pl.pallas_call(sweeps_kernel, in_specs=[INSIDE] + [ANY] * 2 + [INSIDE] *...  20.6 us
    pallas_call x1, Pallas kernels, along_z(): pl.pallas_call(along_z_kernel, in_specs=[ANY, ANY], out_specs=[INSIDE] *...  12.8 us
    ppermute x7, starting transfers between devices, on_device(): lax.ppermute(slots[step], 'wide', [(i, (i + step) % owners) for i in rang...  12.6 us
    pallas_call x1, Pallas kernels, edge_rows(): pl.pallas_call(edge_rows_kernel, in_specs=[INSIDE] * 3 + [ANY] * 4, out_s...  7.02 us
    pallas_call x1, Pallas kernels, interior_y(): pl.pallas_call(interior_y_kernel, in_specs=[INSIDE] * 3 + [ANY], out_spec...  5.63 us
    ppermute x5, starting transfers between devices, trade(): lax.ppermute(second, axis, [(i, (i + 1 if i % 2 else i - 1) % peers) for...  5.04 us
    ppermute x5, starting transfers between devices, trade(): lax.ppermute(first, axis, [(i, i ^ 1) for i in range(peers)])  4.6 us
  transfers between devices with their start and end apart: 17, of which 5 were waited for; matrix products, arithmetic and copies ran while one was open for 0% of the time, Pallas kernels for 22%

profile of v1, /device:TPU:13, one launch (start us, length us, event | category | flops | bytes accessed | tf_op | source)
XLA Modules:
  0.0 106.1 jit_solution(15883036572420967337)
XLA Ops:
  0.6 2.3 %own_faces.1 = (f32[3,64,512]{2,1,0:T(8,128)}, f32[3,64,512]{2,1,0:T(8,128)}, f32[4,96,128]{2,1,0:T(8,128)}, f32[4,96,128]{2,1,0:T(8,128)}) custom-call(f32[32,64,512]{2,1,0:T(8,128)} %core.3), custom_call_target="tpu_custom_call" | custom-call | tf_op jit(solution)/shard_map/own_faces/pallas_call | solution.py:641
  3.0 0.7 collective-permute-start
  3.7 1.3 %collective-permute-start.1 = (f32[3,64,512]{2,1,0:T(8,128)}, f32[3,64,512]{2,1,0:T(8,128)S(1)}, u32[]{:S(2)}, u32[]{:S(2)}) collective-permute-start(f32[3,64,512]{2,1,0:T(8,128)} %get-tuple-element.33), channel_id=1, source_target_pairs={{0,7},{1,2},{2,1},{3,4},{4,3},{5,6},{6,5},{7,0},{8,15},{9,10},{10,... | collective-permute-start | bytes 1179656 | tf_op jit(solution)/shard_map/ppermute | solution.py:685
  5.0 1.2 %collective-permute-start.2 = (f32[4,96,128]{2,1,0:T(8,128)}, f32[4,96,128]{2,1,0:T(8,128)S(1)}, u32[]{:S(2)}, u32[]{:S(2)}) collective-permute-start(f32[4,96,128]{2,1,0:T(8,128)} %get-tuple-element.34), channel_id=1, source_target_pairs={{0,8},{8,0},{16,24},{24,16},{1,9},{9,1},{17,25},{25,17},{2,10},{10... | collective-permute-start | bytes 589832 | tf_op jit(solution)/shard_map/ppermute | solution.py:684
  6.2 0.2 collective-permute-start.3
  6.4 12.8 %along_z.1 = (f32[38,4,80,128]{3,2,1,0:T(8,128)S(1)}, f32[38,4,80,128]{3,2,1,0:T(8,128)S(1)}, bf16[2,32,64,512]{3,2,1,0:T(8,128)(2,1)S(1)}) custom-call(f32[32,64,512]{2,1,0:T(8,128)} %core.3, bf16[3,32,64,512]{3,2,1,0:T(8,128)(2,1)} %u_hbm.1), custom_call_target="tpu_custom_call" | custom-call | flops 62914560 | bytes 8388608 | tf_op jit(solution)/shard_map/along_z/pallas_call | solution.py:134
  19.2 0.0 collective-permute-done.2.ya_hbm
  19.2 0.0 collective-permute-done.3.yb_hbm
  19.2 0.0 collective-permute-done.xa
  19.2 0.0 collective-permute-done.1.xb
  19.2 7.0 %edge_rows.1 = (f32[38,4,80,128]{3,2,1,0:T(8,128)S(1)}, f32[38,4,80,128]{3,2,1,0:T(8,128)S(1)}, f32[4,96,128]{2,1,0:T(8,128)S(1)}, f32[4,96,128]{2,1,0:T(8,128)S(1)}) custom-call(f32[38,4,80,128]{3,2,1,0:T(8,128)S(1)} %get-tuple-element.29.field_in, f32[38,4,80,128]{3,2,1,0:T(8,128)S(1)} %get-tuple-element.30.acc_in, ...), custom_call_target="tpu_custom_call", output_to_operand_aliasing={{0}: (0, {}), {1}: (1, {})} | custom-call | flops 31457280 | bytes 8388608 | tf_op jit(solution)/shard_map/edge_rows/pallas_call | solution.py:387
  26.2 3.1 %edge_planes.1 = (f32[38,4,80,128]{3,2,1,0:T(8,128)S(1)}, f32[3,64,512]{2,1,0:T(8,128)S(1)}, f32[3,64,512]{2,1,0:T(8,128)S(1)}) custom-call(f32[38,4,80,128]{3,2,1,0:T(8,128)S(1)} %get-tuple-element.36.acc_in, f32[38,4,80,128]{3,2,1,0:T(8,128)S(1)} %get-tuple-element.37.field, ...), custom_call_target="tpu_custom_call", output_to_operand_aliasing={{0}: (0, {})} | custom-call | flops 20971520 | bytes 8388608 | tf_op jit(solution)/shard_map/edge_planes/pallas_call | solution.py:404
  29.3 1.1 %collective-permute-start.5 = (f32[3,64,512]{2,1,0:T(8,128)S(1)}, f32[3,64,512]{2,1,0:T(8,128)S(1)}, u32[]{:S(2)}, u32[]{:S(2)}) collective-permute-start(f32[3,64,512]{2,1,0:T(8,128)S(1)} %get-tuple-element.41), channel_id=1, source_target_pairs={{0,7},{1,2},{2,1},{3,4},{4,3},{5,6},{6,5},{7,0},{8,15},{9,10},{10,... | collective-permute-start | bytes 1179656 | tf_op jit(solution)/shard_map/ppermute | solution.py:685
  30.4 0.0 collective-permute-start.4
  30.4 1.2 %collective-permute-start.6 = (f32[4,96,128]{2,1,0:T(8,128)S(1)}, f32[4,96,128]{2,1,0:T(8,128)S(1)}, u32[]{:S(2)}, u32[]{:S(2)}) collective-permute-start(f32[4,96,128]{2,1,0:T(8,128)S(1)} %get-tuple-element.42), channel_id=1, source_target_pairs={{0,8},{8,0},{16,24},{24,16},{1,9},{9,1},{17,25},{25,17},{2,10},{10... | collective-permute-start | bytes 589832 | tf_op jit(solution)/shard_map/ppermute | solution.py:684
  31.7 1.2 %collective-permute-start.7 = (f32[4,96,128]{2,1,0:T(8,128)S(1)}, f32[4,96,128]{2,1,0:T(8,128)S(1)}, u32[]{:S(2)}, u32[]{:S(2)}) collective-permute-start(f32[4,96,128]{2,1,0:T(8,128)S(1)} %get-tuple-element.43), channel_id=1, source_target_pairs={{0,24},{8,16},{16,8},{24,0},{1,25},{9,17},{17,9},{25,1},{2,26},{10... | collective-permute-start | bytes 589832 | tf_op jit(solution)/shard_map/ppermute | solution.py:685
  32.9 5.6 %interior_y.1 = (f32[38,4,80,128]{3,2,1,0:T(8,128)S(1)}, f32[8,128]{1,0:T(8,128)S(1)}) custom-call(f32[38,4,80,128]{3,2,1,0:T(8,128)S(1)} %get-tuple-element.38.acc_in, f32[38,4,80,128]{3,2,1,0:T(8,128)S(1)} %get-tuple-element.37.field, bf16[2,32,64,512]{3,2,1,0:T(8,128)(2,1)S(1)} %get-tuple-element.31.u, ...), custom_call_target="tpu_custom_call", output_to_operand_aliasing={{0}: (0, {})} | custom-call | flops 31457280 | bytes 8388608 | tf_op jit(solution)/shard_map/interior_y/pallas_call | solution.py:418
  38.5 0.0 collective-permute-done.6.ya
  38.5 3.0 %collective-permute-done.7.yb = f32[4,96,128]{2,1,0:T(8,128)S(1)} collective-permute-done((f32[4,96,128]{2,1,0:T(8,128)S(1)}, f32[4,96,128]{2,1,0:T(8,128)S(1)}, u32[]{:S(2)}, u32[]{:S(2)}) %collective-permute-start.7) | collective-permute-done | bytes 196640 | tf_op jit(solution)/shard_map/ppermute | solution.py:685
  41.6 1.4 %collective-permute-start.8 = (f32[4,24,128]{2,1,0:T(8,128)S(1)}, f32[4,24,128]{2,1,0:T(8,128)S(1)}, u32[]{:S(2)}, u32[]{:S(2)}) collective-permute-start(f32[4,24,128]{2,1,0:T(8,128)S(1)} %get-tuple-element.45), channel_id=1, source_target_pairs={{0,1},{1,0},{2,3},{3,2},{4,5},{5,4},{6,7},{7,6},{8,9},{9,8},{10,11... | collective-permute-start | bytes 147464 | tf_op jit(solution)/shard_map/ppermute | solution.py:684
  43.0 1.3 %collective-permute-start.9 = (f32[4,24,128]{2,1,0:T(8,128)S(1)}, f32[4,24,128]{2,1,0:T(8,128)S(1)}, u32[]{:S(2)}, u32[]{:S(2)}) collective-permute-start(f32[4,24,128]{2,1,0:T(8,128)S(1)} %get-tuple-element.46), channel_id=1, source_target_pairs={{0,7},{1,2},{2,1},{3,4},{4,3},{5,6},{6,5},{7,0},{8,15},{9,10},{10,... | collective-permute-start | bytes 147464 | tf_op jit(solution)/shard_map/ppermute | solution.py:685
  44.3 0.0 copy-start
  44.3 0.0 copy-start.1
  44.3 0.0 copy-start.2
  44.3 4.5 %interior_x.1.f0_in = f32[38,4,80,128]{3,2,1,0:T(8,128)S(1)} custom-call(f32[38,4,80,128]{3,2,1,0:T(8,128)S(1)} %get-tuple-element.40.acc_in, f32[38,4,80,128]{3,2,1,0:T(8,128)S(1)} %get-tuple-element.37.field, bf16[2,32,64,512]{3,2,1,0:T(8,128)(2,1)S(1)} %get-tuple-element.31.u), custom_call_target="tpu_custom_call", output_to_operand_aliasing={{}: (0, {})} | custom-call | flops 31457280 | bytes 8388608 | tf_op jit(solution)/shard_map/interior_x/pallas_call | solution.py:432
  48.8 0.0 collective-permute-done.8.ca
  48.8 0.0 collective-permute-done.9.cb
  48.8 0.0 collective-permute-done.5.xb
  48.8 0.0 collective-permute-done.4.xa
  48.9 0.0 copy-done
  48.9 0.0 copy-done.1
  48.9 0.0 copy-done.2
  48.9 20.6 %sweeps.1 = (f32[38,4,80,128]{3,2,1,0:T(8,128)S(1)}, f32[32,64,512]{2,1,0:T(8,128)}, f32[80,512]{1,0:T(8,128)S(1)}, f32[80,512]{1,0:T(8,128)S(1)}, f32[80,512]{1...) custom-call(f32[38,4,80,128]{3,2,1,0:T(8,128)S(1)} %interior_x.1.f0_, ...), custom_call_target="tpu_custom_call", output_to_operand_aliasing={{0}: (0, {})} | custom-call | flops 104857600 | bytes 8388608 | tf_op jit(solution)/shard_map/sweeps/pallas_call | solution.py:592
  69.5 0.5 collective-permute-start.10
  70.0 2.7 %collective-permute-start.11 = (f32[80,512]{1,0:T(8,128)S(1)}, f32[80,512]{1,0:T(8,128)S(1)}, u32[]{:S(2)}, u32[]{:S(2)}) collective-permute-start(f32[80,512]{1,0:T(8,128)S(1)} %get-tuple-element.50), channel_id=1, source_target_pairs={{0,2},{1,3},{2,4},{3,5},{4,6},{5,7},{6,0},{7,1},{8,10},{9,11},{10,... | collective-permute-start | bytes 491528 | tf_op jit(solution)/shard_map/ppermute | solution.py:709
  72.7 3.6 %collective-permute-start.12 = (f32[80,512]{1,0:T(8,128)S(1)}, f32[80,512]{1,0:T(8,128)S(1)}, u32[]{:S(2)}, u32[]{:S(2)}) collective-permute-start(f32[80,512]{1,0:T(8,128)S(1)} %get-tuple-element.51), channel_id=1, source_target_pairs={{0,3},{1,4},{2,5},{3,6},{4,7},{5,0},{6,1},{7,2},{8,11},{9,12},{10,... | collective-permute-start | bytes 491528 | tf_op jit(solution)/shard_map/ppermute | solution.py:709
  76.2 0.0 collective-permute-start.13
  76.3 1.7 %collective-permute-start.14 = (f32[80,512]{1,0:T(8,128)S(1)}, f32[80,512]{1,0:T(8,128)S(1)}, u32[]{:S(2)}, u32[]{:S(2)}) collective-permute-start(f32[80,512]{1,0:T(8,128)S(1)} %get-tuple-element.53), channel_id=1, source_target_pairs={{0,5},{1,6},{2,7},{3,0},{4,1},{5,2},{6,3},{7,4},{8,13},{9,14},{10,... | collective-permute-start | bytes 491528 | tf_op jit(solution)/shard_map/ppermute | solution.py:709
  77.9 0.0 collective-permute-done.10.refs_1_
  77.9 2.4 %collective-permute-start.15 = (f32[80,512]{1,0:T(8,128)S(1)}, f32[80,512]{1,0:T(8,128)S(1)}, u32[]{:S(2)}, u32[]{:S(2)}) collective-permute-start(f32[80,512]{1,0:T(8,128)S(1)} %get-tuple-element.54), channel_id=1, source_target_pairs={{0,6},{1,7},{2,0},{3,1},{4,2},{5,3},{6,4},{7,5},{8,14},{9,15},{10,... | collective-permute-start | bytes 491528 | tf_op jit(solution)/shard_map/ppermute | solution.py:709
  80.3 0.0 collective-permute-done.11.refs_2_
  80.3 1.7 %collective-permute-start.16 = (f32[80,512]{1,0:T(8,128)S(1)}, f32[80,512]{1,0:T(8,128)S(1)}, u32[]{:S(2)}, u32[]{:S(2)}) collective-permute-start(f32[80,512]{1,0:T(8,128)S(1)} %get-tuple-element.55), channel_id=1, source_target_pairs={{0,7},{1,0},{2,1},{3,2},{4,3},{5,4},{6,5},{7,6},{8,15},{9,8},{10,9... | collective-permute-start | bytes 491528 | tf_op jit(solution)/shard_map/ppermute | solution.py:709
  82.0 0.1 collective-permute-done.12.refs_3_
  82.2 15.2 %collective-permute-done.13.refs_4_ = f32[80,512]{1,0:T(8,128)S(1)} collective-permute-done((f32[80,512]{1,0:T(8,128)S(1)}, f32[80,512]{1,0:T(8,128)S(1)}, u32[]{:S(2)}, u32[]{:S(2)}) %collective-permute-start.13) | collective-permute-done | bytes 163872 | tf_op jit(solution)/shard_map/ppermute | solution.py:709
  97.3 0.0 collective-permute-done.14.refs_5_
  97.3 7.6 %collective-permute-done.15.refs_6_ = f32[80,512]{1,0:T(8,128)S(1)} collective-permute-done((f32[80,512]{1,0:T(8,128)S(1)}, f32[80,512]{1,0:T(8,128)S(1)}, u32[]{:S(2)}, u32[]{:S(2)}) %collective-permute-start.15) | collective-permute-done | bytes 163872 | tf_op jit(solution)/shard_map/ppermute | solution.py:709
  104.9 0.1 collective-permute-done.16.refs_7_
  105.0 1.1 %gather_blocks.1 = f32[8,80,512]{2,1,0:T(8,128)} custom-call(f32[80,512]{1,0:T(8,128)S(1)} %get-tuple-element.48.refs_0_, f32[80,512]{1,0:T(8,128)S(1)} %collective-permute-done.10.refs_1_, f32[80,512]{1,0:T(8,128)S(1)} %collective-permute-done.11.refs_2_, f32[80,512]{1,0:T(8,128)S(1)} %collective-permute-done.12.refs_3_, ...), custom_call_target="tpu_custom_call" | custom-call | tf_op jit(solution)/shard_map/gather_blocks/pallas_call | solution.py:670
  (1 shorter events, 0.0 us)
Async XLA Ops:
  3.0 16.2 %collective-permute-start = (f32[3,64,512]{2,1,0:T(8,128)}, f32[3,64,512]{2,1,0:T(8,128)S(1)}, u32[]{:S(2)}, u32[]{:S(2)}) collective-permute-start(f32[3,64,512]{2,1,0:T(8,128)} %get-tuple-element.32), channel_id=1, source_target_pairs={{0,1},{1,0},{2,3},{3,2},{4,5},{5,4},{6,7},{7,6},{8,9},{9,8},{10,11... | collective-permute-start | bytes 1179656 | tf_op jit(solution)/shard_map/ppermute | solution.py:684
  3.7 15.5 %collective-permute-start.1 = (f32[3,64,512]{2,1,0:T(8,128)}, f32[3,64,512]{2,1,0:T(8,128)S(1)}, u32[]{:S(2)}, u32[]{:S(2)}) collective-permute-start(f32[3,64,512]{2,1,0:T(8,128)} %get-tuple-element.33), channel_id=1, source_target_pairs={{0,7},{1,2},{2,1},{3,4},{4,3},{5,6},{6,5},{7,0},{8,15},{9,10},{10,... | collective-permute-start | bytes 1179656 | tf_op jit(solution)/shard_map/ppermute | solution.py:685
  5.0 14.2 %collective-permute-start.2 = (f32[4,96,128]{2,1,0:T(8,128)}, f32[4,96,128]{2,1,0:T(8,128)S(1)}, u32[]{:S(2)}, u32[]{:S(2)}) collective-permute-start(f32[4,96,128]{2,1,0:T(8,128)} %get-tuple-element.34), channel_id=1, source_target_pairs={{0,8},{8,0},{16,24},{24,16},{1,9},{9,1},{17,25},{25,17},{2,10},{10... | collective-permute-start | bytes 589832 | tf_op jit(solution)/shard_map/ppermute | solution.py:684
  6.2 13.0 %collective-permute-start.3 = (f32[4,96,128]{2,1,0:T(8,128)}, f32[4,96,128]{2,1,0:T(8,128)S(1)}, u32[]{:S(2)}, u32[]{:S(2)}) collective-permute-start(f32[4,96,128]{2,1,0:T(8,128)} %get-tuple-element.35), channel_id=1, source_target_pairs={{0,24},{8,16},{16,8},{24,0},{1,25},{9,17},{17,9},{25,1},{2,26},{10... | collective-permute-start | bytes 589832 | tf_op jit(solution)/shard_map/ppermute | solution.py:685
  29.3 19.5 %collective-permute-start.5 = (f32[3,64,512]{2,1,0:T(8,128)S(1)}, f32[3,64,512]{2,1,0:T(8,128)S(1)}, u32[]{:S(2)}, u32[]{:S(2)}) collective-permute-start(f32[3,64,512]{2,1,0:T(8,128)S(1)} %get-tuple-element.41), channel_id=1, source_target_pairs={{0,7},{1,2},{2,1},{3,4},{4,3},{5,6},{6,5},{7,0},{8,15},{9,10},{10,... | collective-permute-start | bytes 1179656 | tf_op jit(solution)/shard_map/ppermute | solution.py:685
  30.4 18.4 %collective-permute-start.4 = (f32[3,64,512]{2,1,0:T(8,128)S(1)}, f32[3,64,512]{2,1,0:T(8,128)S(1)}, u32[]{:S(2)}, u32[]{:S(2)}) collective-permute-start(f32[3,64,512]{2,1,0:T(8,128)S(1)} %get-tuple-element.39.after), channel_id=1, source_target_pairs={{0,1},{1,0},{2,3},{3,2},{4,5},{5,4},{6,7},{7,6},{8,9},{9,8},{10,11... | collective-permute-start | bytes 1179656 | tf_op jit(solution)/shard_map/ppermute | solution.py:684
  30.4 8.1 %collective-permute-start.6 = (f32[4,96,128]{2,1,0:T(8,128)S(1)}, f32[4,96,128]{2,1,0:T(8,128)S(1)}, u32[]{:S(2)}, u32[]{:S(2)}) collective-permute-start(f32[4,96,128]{2,1,0:T(8,128)S(1)} %get-tuple-element.42), channel_id=1, source_target_pairs={{0,8},{8,0},{16,24},{24,16},{1,9},{9,1},{17,25},{25,17},{2,10},{10... | collective-permute-start | bytes 589832 | tf_op jit(solution)/shard_map/ppermute | solution.py:684
  31.7 9.9 %collective-permute-start.7 = (f32[4,96,128]{2,1,0:T(8,128)S(1)}, f32[4,96,128]{2,1,0:T(8,128)S(1)}, u32[]{:S(2)}, u32[]{:S(2)}) collective-permute-start(f32[4,96,128]{2,1,0:T(8,128)S(1)} %get-tuple-element.43), channel_id=1, source_target_pairs={{0,24},{8,16},{16,8},{24,0},{1,25},{9,17},{17,9},{25,1},{2,26},{10... | collective-permute-start | bytes 589832 | tf_op jit(solution)/shard_map/ppermute | solution.py:685
  41.6 7.2 %collective-permute-start.8 = (f32[4,24,128]{2,1,0:T(8,128)S(1)}, f32[4,24,128]{2,1,0:T(8,128)S(1)}, u32[]{:S(2)}, u32[]{:S(2)}) collective-permute-start(f32[4,24,128]{2,1,0:T(8,128)S(1)} %get-tuple-element.45), channel_id=1, source_target_pairs={{0,1},{1,0},{2,3},{3,2},{4,5},{5,4},{6,7},{7,6},{8,9},{9,8},{10,11... | collective-permute-start | bytes 147464 | tf_op jit(solution)/shard_map/ppermute | solution.py:684
  43.0 5.8 %collective-permute-start.9 = (f32[4,24,128]{2,1,0:T(8,128)S(1)}, f32[4,24,128]{2,1,0:T(8,128)S(1)}, u32[]{:S(2)}, u32[]{:S(2)}) collective-permute-start(f32[4,24,128]{2,1,0:T(8,128)S(1)} %get-tuple-element.46), channel_id=1, source_target_pairs={{0,7},{1,2},{2,1},{3,4},{4,3},{5,6},{6,5},{7,0},{8,15},{9,10},{10,... | collective-permute-start | bytes 147464 | tf_op jit(solution)/shard_map/ppermute | solution.py:685
  44.3 4.6 %copy-start = (bf16[512,512]{1,0:T(8,128)(2,1)S(1)}, bf16[512,512]{1,0:T(8,128)(2,1)}, u32[]{:S(2)}) copy-start(bf16[512,512]{1,0:T(8,128)(2,1)} %constant.4.clone.perm_ref) | copy-start | bytes 1572868
  44.3 4.6 %copy-start.1 = (bf16[256,512]{1,0:T(8,128)(2,1)S(1)}, bf16[256,512]{1,0:T(8,128)(2,1)}, u32[]{:S(2)}) copy-start(bf16[256,512]{1,0:T(8,128)(2,1)} %constant.5.clone.zmean_ref) | copy-start | bytes 786436
  44.3 4.6 %copy-start.2 = (s32[1,1,256,1]{2,3,1,0:T(1,128)S(1)}, s32[1,1,256,1]{2,3,1,0:T(1,128)}, u32[]{:S(2)}) copy-start(s32[1,1,256,1]{2,3,1,0:T(1,128)} %param.7) | copy-start | bytes 3076
  69.5 8.5 %collective-permute-start.10 = (f32[80,512]{1,0:T(8,128)S(1)}, f32[80,512]{1,0:T(8,128)S(1)}, u32[]{:S(2)}, u32[]{:S(2)}) collective-permute-start(f32[80,512]{1,0:T(8,128)S(1)} %get-tuple-element.49), channel_id=1, source_target_pairs={{0,1},{1,2},{2,3},{3,4},{4,5},{5,6},{6,7},{7,0},{8,9},{9,10},{10,1... | collective-permute-start | bytes 491528 | tf_op jit(solution)/shard_map/ppermute | solution.py:709
  70.0 10.3 %collective-permute-start.11 = (f32[80,512]{1,0:T(8,128)S(1)}, f32[80,512]{1,0:T(8,128)S(1)}, u32[]{:S(2)}, u32[]{:S(2)}) collective-permute-start(f32[80,512]{1,0:T(8,128)S(1)} %get-tuple-element.50), channel_id=1, source_target_pairs={{0,2},{1,3},{2,4},{3,5},{4,6},{5,7},{6,0},{7,1},{8,10},{9,11},{10,... | collective-permute-start | bytes 491528 | tf_op jit(solution)/shard_map/ppermute | solution.py:709
  72.7 9.5 %collective-permute-start.12 = (f32[80,512]{1,0:T(8,128)S(1)}, f32[80,512]{1,0:T(8,128)S(1)}, u32[]{:S(2)}, u32[]{:S(2)}) collective-permute-start(f32[80,512]{1,0:T(8,128)S(1)} %get-tuple-element.51), channel_id=1, source_target_pairs={{0,3},{1,4},{2,5},{3,6},{4,7},{5,0},{6,1},{7,2},{8,11},{9,12},{10,... | collective-permute-start | bytes 491528 | tf_op jit(solution)/shard_map/ppermute | solution.py:709
  76.2 21.1 %collective-permute-start.13 = (f32[80,512]{1,0:T(8,128)S(1)}, f32[80,512]{1,0:T(8,128)S(1)}, u32[]{:S(2)}, u32[]{:S(2)}) collective-permute-start(f32[80,512]{1,0:T(8,128)S(1)} %get-tuple-element.52), channel_id=1, source_target_pairs={{0,4},{1,5},{2,6},{3,7},{4,0},{5,1},{6,2},{7,3},{8,12},{9,13},{10,... | collective-permute-start | bytes 491528 | tf_op jit(solution)/shard_map/ppermute | solution.py:709
  76.3 21.1 %collective-permute-start.14 = (f32[80,512]{1,0:T(8,128)S(1)}, f32[80,512]{1,0:T(8,128)S(1)}, u32[]{:S(2)}, u32[]{:S(2)}) collective-permute-start(f32[80,512]{1,0:T(8,128)S(1)} %get-tuple-element.53), channel_id=1, source_target_pairs={{0,5},{1,6},{2,7},{3,0},{4,1},{5,2},{6,3},{7,4},{8,13},{9,14},{10,... | collective-permute-start | bytes 491528 | tf_op jit(solution)/shard_map/ppermute | solution.py:709
  77.9 27.0 %collective-permute-start.15 = (f32[80,512]{1,0:T(8,128)S(1)}, f32[80,512]{1,0:T(8,128)S(1)}, u32[]{:S(2)}, u32[]{:S(2)}) collective-permute-start(f32[80,512]{1,0:T(8,128)S(1)} %get-tuple-element.54), channel_id=1, source_target_pairs={{0,6},{1,7},{2,0},{3,1},{4,2},{5,3},{6,4},{7,5},{8,14},{9,15},{10,... | collective-permute-start | bytes 491528 | tf_op jit(solution)/shard_map/ppermute | solution.py:709
  80.3 24.7 %collective-permute-start.16 = (f32[80,512]{1,0:T(8,128)S(1)}, f32[80,512]{1,0:T(8,128)S(1)}, u32[]{:S(2)}, u32[]{:S(2)}) collective-permute-start(f32[80,512]{1,0:T(8,128)S(1)} %get-tuple-element.55), channel_id=1, source_target_pairs={{0,7},{1,0},{2,1},{3,2},{4,3},{5,4},{6,5},{7,6},{8,15},{9,8},{10,9... | collective-permute-start | bytes 491528 | tf_op jit(solution)/shard_map/ppermute | solution.py:709

commit v2 on v1

--- a/solution.py
+++ b/solution.py
@@ -1,4 +1,3 @@
-import functools
 import math
 import jax
 import jax.numpy as jnp
@@ -54,23 +53,36 @@
 def along_z_kernel(core, u_hbm, field, acc, u, uz, ft, ut, es, us, ws, vs, hs, sem):
     nx, ny, nz = core.shape
     copies = Copies(sem)
-    bounds = [0, nx // 16, nx // 4, nx // 2, 3 * nx // 4, nx]
-    groups = list(zip(bounds, bounds[1:]))
+    per = LANES // ny
+    step = 2 * per
+    bounds = [0, step, 2 * step, nx // 2, nx]
+    groups = [(x0, x1) for x0, x1 in zip(bounds, bounds[1:]) if x1 > x0]
     for x0, x1 in groups:
         xs = pl.ds(x0, x1 - x0)
         for k, lanes in lane_chunks(nz):
             copies.start(x0, core.at[xs, :, lanes], field.at[pl.ds(x0 + RIM, x1 - x0), k, pl.ds(ROWS, ny), :])
         copies.start(x0, u_hbm.at[2, xs], uz.at[xs])
     copies.start("u", u_hbm.at[pl.ds(0, 2)], u)
-    per = LANES // ny
-    for x0, x1 in groups:
-        copies.wait(x0)
-        lax.fori_loop(x0 // per, x1 // per, functools.partial(z_planes, field, uz, acc, ft, ut, (es, us, ws, vs, hs), per), 0)
+    streams = (es, us, ws, vs, hs)
+    first, second = (ft.at[0], ut.at[0]), (ft.at[1], ut.at[1])
+
+    def two(j, carry):
+        turn_in(field, uz, *second, per, 2 * j + 1)
+        z_planes(field, acc, *first, streams, per, 2 * j)
+        turn_in(field, uz, *first, per, jnp.minimum(2 * j + 2, nx // per - 1))
+        z_planes(field, acc, *second, streams, per, 2 * j + 1)
+        return carry
+
+    copies.wait(0)
+    turn_in(field, uz, *first, per, 0)
+    for g, (x0, x1) in enumerate(groups):
+        if g + 1 < len(groups):
+            copies.wait(groups[g + 1][0])
+        lax.fori_loop(x0 // step, x1 // step, two, 0)
     copies.finish()
 
 
-def z_planes(field, uz, acc, ft, ut, streams, per, i, carry):
-    es, us, ws, vs, hs = streams
+def turn_in(field, uz, ft, ut, per, i):
     ny = LANES // per
     n = field.shape[1]
     depth = n * LANES
@@ -82,6 +94,15 @@
         ut[pl.ds(k * LANES, LANES), :] = v.astype(jnp.float32).T
     ft[pl.ds(0, ROWS), :] = jnp.broadcast_to(ft[pl.ds(ROWS, 1), :], (ROWS, LANES))
     ft[pl.ds(ROWS + depth, ROWS), :] = jnp.broadcast_to(ft[pl.ds(ROWS + depth - 1, 1), :], (ROWS, LANES))
+
+
+def z_planes(field, acc, ft, ut, streams, per, i):
+    es, us, ws, vs, hs = streams
+    ny = LANES // per
+    n = field.shape[1]
+    depth = n * LANES
+    rows = pl.ds(ROWS, ny)
+    planes = [per * i + p for p in range(per)]
 
     def at(z):
         return ft[pl.ds(ROWS + z, ROWS), :]
@@ -117,7 +138,6 @@
         change = ut[pl.ds(k * LANES, LANES), :].T
         for p, x in enumerate(planes):
             acc[x + RIM, k, rows, :] = field[x + RIM, k, rows, :] - change[p * ny : (p + 1) * ny, :]
-    return carry
 
 
 def in_vmem(shape, dtype=jnp.float32):
@@ -138,8 +158,8 @@
         out_shape=[rimmed(level_set.shape)] * 2 + [in_vmem((2, nx, ny, nz), velocity.dtype)],
         scratch_shapes=[
             pltpu.VMEM((nx, ny, nz), velocity.dtype),
-            pltpu.VMEM((nz + 2 * ROWS, LANES), jnp.float32),
-            pltpu.VMEM((nz, LANES), jnp.float32),
+            pltpu.VMEM((2, nz + 2 * ROWS, LANES), jnp.float32),
+            pltpu.VMEM((2, nz, LANES), jnp.float32),
         ]
         + [pltpu.VMEM((nz + 3 * ROWS, LANES), jnp.float32)] * 5
         + [pltpu.SemaphoreType.DMA((40,))],
@@ -264,7 +284,7 @@
 
 def side_shape(shape):
     nx, _, nz = shape
-    return (nz // LANES, RIM * nx, LANES)
+    return (nz // LANES, RIM * nx + ROWS, LANES)
 
 
 def first_is_above(axis):
@@ -443,7 +463,7 @@
 
 def corner_kernel(ya, yb, token, ca, cb):
     n, rows, _ = ya.shape
-    faces, _ = face_starts(rows // RIM)
+    faces, _ = face_starts((rows - ROWS) // RIM)
     for k in range(n):
         for out, face in ((ca, faces[0]), (cb, faces[1])):
             for i in range(RIM):
@@ -457,7 +477,7 @@
         corner_kernel,
         in_specs=[INSIDE] * 3,
         out_specs=[INSIDE] * 2,
-        out_shape=[shapes(ya.shape[0], 3 * ROWS, LANES)] * 2,
+        out_shape=[shapes(ya.shape[0], 4 * ROWS, LANES)] * 2,
         name="corner_faces",
         compiler_params=pltpu.CompilerParams(vmem_limit_bytes=4 * MIB),
     )(ya, yb, token)

time: 106 us -> 106 us (level)
  the two profiles are of different devices: /device:TPU:13 before, /device:TPU:11 now
where the time goes in v2:
time: 106 us
  Pallas kernels  56.2 us (53%)
  waiting for transfers between devices  26.7 us (25%)
  starting transfers between devices  22.2 us (21%)
    ppermute x7, waiting for transfers between devices, on_device(): lax.ppermute(slots[step], 'wide', [(i, (i + step) % owners) for i in rang...  22.9 us
    pallas_call x1, Pallas kernels, sweeps(): pl.pallas_call(sweeps_kernel, in_specs=[INSIDE] + [ANY] * 2 + [INSIDE] *...  20.6 us
    ppermute x7, starting transfers between devices, on_device(): lax.ppermute(slots[step], 'wide', [(i, (i + step) % owners) for i in rang...  12.6 us
    pallas_call x1, Pallas kernels, along_z(): pl.pallas_call(along_z_kernel, in_specs=[ANY, ANY], out_specs=[INSIDE] *...  11.8 us
    pallas_call x1, Pallas kernels, edge_rows(): pl.pallas_call(edge_rows_kernel, in_specs=[INSIDE] * 3 + [ANY] * 4, out_s...  7.06 us
    ppermute x5, starting transfers between devices, trade(): lax.ppermute(second, axis, [(i, (i + 1 if i % 2 else i - 1) % peers) for...  6.95 us
    pallas_call x1, Pallas kernels, interior_y(): pl.pallas_call(interior_y_kernel, in_specs=[INSIDE] * 3 + [ANY], out_spec...  5.63 us
    pallas_call x1, Pallas kernels, interior_x(): pl.pallas_call(interior_x_kernel, in_specs=[INSIDE] * 3, out_specs=INSIDE...  4.52 us
  transfers between devices with their start and end apart: 17, of which 5 were waited for; matrix products, arithmetic and copies ran while one was open for 0% of the time, Pallas kernels for 21%

profile of v2, /device:TPU:11, one launch (start us, length us, event | category | flops | bytes accessed | tf_op | source)
XLA Modules:
  0.0 105.9 jit_solution(8183500571575962283)
XLA Ops:
  0.6 2.3 %own_faces.1 = (f32[3,64,512]{2,1,0:T(8,128)}, f32[3,64,512]{2,1,0:T(8,128)}, f32[4,104,128]{2,1,0:T(8,128)}, f32[4,104,128]{2,1,0:T(8,128)}) custom-call(f32[32,64,512]{2,1,0:T(8,128)} %core.3), custom_call_target="tpu_custom_call" | custom-call | tf_op jit(solution)/shard_map/own_faces/pallas_call | solution.py:661
  3.0 0.7 collective-permute-start
  3.7 1.3 %collective-permute-start.1 = (f32[3,64,512]{2,1,0:T(8,128)}, f32[3,64,512]{2,1,0:T(8,128)S(1)}, u32[]{:S(2)}, u32[]{:S(2)}) collective-permute-start(f32[3,64,512]{2,1,0:T(8,128)} %get-tuple-element.33), channel_id=1, source_target_pairs={{0,7},{1,2},{2,1},{3,4},{4,3},{5,6},{6,5},{7,0},{8,15},{9,10},{10,... | collective-permute-start | bytes 1179656 | tf_op jit(solution)/shard_map/ppermute | solution.py:705
  5.0 0.3 collective-permute-start.2
  5.2 2.2 %collective-permute-start.3 = (f32[4,104,128]{2,1,0:T(8,128)}, f32[4,104,128]{2,1,0:T(8,128)S(1)}, u32[]{:S(2)}, u32[]{:S(2)}) collective-permute-start(f32[4,104,128]{2,1,0:T(8,128)} %get-tuple-element.35), channel_id=1, source_target_pairs={{0,24},{8,16},{16,8},{24,0},{1,25},{9,17},{17,9},{25,1},{2,26},{10... | collective-permute-start | bytes 638984 | tf_op jit(solution)/shard_map/ppermute | solution.py:705
  7.4 11.8 %along_z.1 = (f32[38,4,80,128]{3,2,1,0:T(8,128)S(1)}, f32[38,4,80,128]{3,2,1,0:T(8,128)S(1)}, bf16[2,32,64,512]{3,2,1,0:T(8,128)(2,1)S(1)}) custom-call(f32[32,64,512]{2,1,0:T(8,128)} %core.3, bf16[3,32,64,512]{3,2,1,0:T(8,128)(2,1)} %u_hbm.1), custom_call_target="tpu_custom_call" | custom-call | flops 62914560 | bytes 8388608 | tf_op jit(solution)/shard_map/along_z/pallas_call | solution.py:154
  19.2 0.0 collective-permute-done.2.ya_hbm
  19.3 0.0 collective-permute-done.3.yb_hbm
  19.3 0.0 collective-permute-done.xa
  19.3 0.0 collective-permute-done.1.xb
  19.3 7.1 %edge_rows.1 = (f32[38,4,80,128]{3,2,1,0:T(8,128)S(1)}, f32[38,4,80,128]{3,2,1,0:T(8,128)S(1)}, f32[4,104,128]{2,1,0:T(8,128)S(1)}, f32[4,104,128]{2,1,0:T(8,128)S(1)}) custom-call(f32[38,4,80,128]{3,2,1,0:T(8,128)S(1)} %get-tuple-element.29.field_in, f32[38,4,80,128]{3,2,1,0:T(8,128)S(1)} %get-tuple-element.30.acc_in, ...), custom_call_target="tpu_custom_call", output_to_operand_aliasing={{0}: (0, {}), {1}: (1, {})} | custom-call | flops 31457280 | bytes 8388608 | tf_op jit(solution)/shard_map/edge_rows/pallas_call | solution.py:407
  26.3 3.1 %edge_planes.1 = (f32[38,4,80,128]{3,2,1,0:T(8,128)S(1)}, f32[3,64,512]{2,1,0:T(8,128)S(1)}, f32[3,64,512]{2,1,0:T(8,128)S(1)}) custom-call(f32[38,4,80,128]{3,2,1,0:T(8,128)S(1)} %get-tuple-element.36.acc_in, f32[38,4,80,128]{3,2,1,0:T(8,128)S(1)} %get-tuple-element.37.field, ...), custom_call_target="tpu_custom_call", output_to_operand_aliasing={{0}: (0, {})} | custom-call | flops 20971520 | bytes 8388608 | tf_op jit(solution)/shard_map/edge_planes/pallas_call | solution.py:424
  29.4 1.1 %collective-permute-start.5 = (f32[3,64,512]{2,1,0:T(8,128)S(1)}, f32[3,64,512]{2,1,0:T(8,128)S(1)}, u32[]{:S(2)}, u32[]{:S(2)}) collective-permute-start(f32[3,64,512]{2,1,0:T(8,128)S(1)} %get-tuple-element.41), channel_id=1, source_target_pairs={{0,7},{1,2},{2,1},{3,4},{4,3},{5,6},{6,5},{7,0},{8,15},{9,10},{10,... | collective-permute-start | bytes 1179656 | tf_op jit(solution)/shard_map/ppermute | solution.py:705
  30.6 0.0 collective-permute-start.4
  30.6 0.3 collective-permute-start.6
  30.8 1.2 %collective-permute-start.7 = (f32[4,104,128]{2,1,0:T(8,128)S(1)}, f32[4,104,128]{2,1,0:T(8,128)S(1)}, u32[]{:S(2)}, u32[]{:S(2)}) collective-permute-start(f32[4,104,128]{2,1,0:T(8,128)S(1)} %get-tuple-element.43), channel_id=1, source_target_pairs={{0,24},{8,16},{16,8},{24,0},{1,25},{9,17},{17,9},{25,1},{2,26},{10... | collective-permute-start | bytes 638984 | tf_op jit(solution)/shard_map/ppermute | solution.py:705
  32.0 5.6 %interior_y.1 = (f32[38,4,80,128]{3,2,1,0:T(8,128)S(1)}, f32[8,128]{1,0:T(8,128)S(1)}) custom-call(f32[38,4,80,128]{3,2,1,0:T(8,128)S(1)} %get-tuple-element.38.acc_in, f32[38,4,80,128]{3,2,1,0:T(8,128)S(1)} %get-tuple-element.37.field, bf16[2,32,64,512]{3,2,1,0:T(8,128)(2,1)S(1)} %get-tuple-element.31.u, ...), custom_call_target="tpu_custom_call", output_to_operand_aliasing={{0}: (0, {})} | custom-call | flops 31457280 | bytes 8388608 | tf_op jit(solution)/shard_map/interior_y/pallas_call | solution.py:438
  37.6 0.0 collective-permute-done.6.ya
  37.6 3.7 %collective-permute-done.7.yb = f32[4,104,128]{2,1,0:T(8,128)S(1)} collective-permute-done((f32[4,104,128]{2,1,0:T(8,128)S(1)}, f32[4,104,128]{2,1,0:T(8,128)S(1)}, u32[]{:S(2)}, u32[]{:S(2)}) %collective-permute-start.7) | collective-permute-done | bytes 213024 | tf_op jit(solution)/shard_map/ppermute | solution.py:705
  41.4 1.4 %collective-permute-start.8 = (f32[4,32,128]{2,1,0:T(8,128)S(1)}, f32[4,32,128]{2,1,0:T(8,128)S(1)}, u32[]{:S(2)}, u32[]{:S(2)}) collective-permute-start(f32[4,32,128]{2,1,0:T(8,128)S(1)} %get-tuple-element.45), channel_id=1, source_target_pairs={{0,1},{1,0},{2,3},{3,2},{4,5},{5,4},{6,7},{7,6},{8,9},{9,8},{10,11... | collective-permute-start | bytes 196616 | tf_op jit(solution)/shard_map/ppermute | solution.py:704
  42.8 1.3 %collective-permute-start.9 = (f32[4,32,128]{2,1,0:T(8,128)S(1)}, f32[4,32,128]{2,1,0:T(8,128)S(1)}, u32[]{:S(2)}, u32[]{:S(2)}) collective-permute-start(f32[4,32,128]{2,1,0:T(8,128)S(1)} %get-tuple-element.46), channel_id=1, source_target_pairs={{0,7},{1,2},{2,1},{3,4},{4,3},{5,6},{6,5},{7,0},{8,15},{9,10},{10,... | collective-permute-start | bytes 196616 | tf_op jit(solution)/shard_map/ppermute | solution.py:705
  44.1 0.0 copy-start
  44.1 0.0 copy-start.1
  44.1 0.0 copy-start.2
  44.1 4.5 %interior_x.1.f0_in = f32[38,4,80,128]{3,2,1,0:T(8,128)S(1)} custom-call(f32[38,4,80,128]{3,2,1,0:T(8,128)S(1)} %get-tuple-element.40.acc_in, f32[38,4,80,128]{3,2,1,0:T(8,128)S(1)} %get-tuple-element.37.field, bf16[2,32,64,512]{3,2,1,0:T(8,128)(2,1)S(1)} %get-tuple-element.31.u), custom_call_target="tpu_custom_call", output_to_operand_aliasing={{}: (0, {})} | custom-call | flops 31457280 | bytes 8388608 | tf_op jit(solution)/shard_map/interior_x/pallas_call | solution.py:452
  48.6 0.0 collective-permute-done.8.ca
  48.6 0.0 collective-permute-done.9.cb
  48.6 0.0 collective-permute-done.5.xb
  48.6 0.0 collective-permute-done.4.xa
  48.6 0.0 copy-done
  48.7 0.0 copy-done.1
  48.7 0.0 copy-done.2
  48.7 20.6 %sweeps.1 = (f32[38,4,80,128]{3,2,1,0:T(8,128)S(1)}, f32[32,64,512]{2,1,0:T(8,128)}, f32[80,512]{1,0:T(8,128)S(1)}, f32[80,512]{1,0:T(8,128)S(1)}, f32[80,512]{1...) custom-call(f32[38,4,80,128]{3,2,1,0:T(8,128)S(1)} %interior_x.1.f0_, ...), custom_call_target="tpu_custom_call", output_to_operand_aliasing={{0}: (0, {})} | custom-call | flops 104857600 | bytes 8388608 | tf_op jit(solution)/shard_map/sweeps/pallas_call | solution.py:612
  69.3 0.5 collective-permute-start.10
  69.8 2.7 %collective-permute-start.11 = (f32[80,512]{1,0:T(8,128)S(1)}, f32[80,512]{1,0:T(8,128)S(1)}, u32[]{:S(2)}, u32[]{:S(2)}) collective-permute-start(f32[80,512]{1,0:T(8,128)S(1)} %get-tuple-element.50), channel_id=1, source_target_pairs={{0,2},{1,3},{2,4},{3,5},{4,6},{5,7},{6,0},{7,1},{8,10},{9,11},{10,... | collective-permute-start | bytes 491528 | tf_op jit(solution)/shard_map/ppermute | solution.py:729
  72.5 3.6 %collective-permute-start.12 = (f32[80,512]{1,0:T(8,128)S(1)}, f32[80,512]{1,0:T(8,128)S(1)}, u32[]{:S(2)}, u32[]{:S(2)}) collective-permute-start(f32[80,512]{1,0:T(8,128)S(1)} %get-tuple-element.51), channel_id=1, source_target_pairs={{0,3},{1,4},{2,5},{3,6},{4,7},{5,0},{6,1},{7,2},{8,11},{9,12},{10,... | collective-permute-start | bytes 491528 | tf_op jit(solution)/shard_map/ppermute | solution.py:729
  76.1 0.0 collective-permute-start.13
  76.1 1.7 %collective-permute-start.14 = (f32[80,512]{1,0:T(8,128)S(1)}, f32[80,512]{1,0:T(8,128)S(1)}, u32[]{:S(2)}, u32[]{:S(2)}) collective-permute-start(f32[80,512]{1,0:T(8,128)S(1)} %get-tuple-element.53), channel_id=1, source_target_pairs={{0,5},{1,6},{2,7},{3,0},{4,1},{5,2},{6,3},{7,4},{8,13},{9,14},{10,... | collective-permute-start | bytes 491528 | tf_op jit(solution)/shard_map/ppermute | solution.py:729
  77.8 0.0 collective-permute-done.10.refs_1_
  77.8 2.4 %collective-permute-start.15 = (f32[80,512]{1,0:T(8,128)S(1)}, f32[80,512]{1,0:T(8,128)S(1)}, u32[]{:S(2)}, u32[]{:S(2)}) collective-permute-start(f32[80,512]{1,0:T(8,128)S(1)} %get-tuple-element.54), channel_id=1, source_target_pairs={{0,6},{1,7},{2,0},{3,1},{4,2},{5,3},{6,4},{7,5},{8,14},{9,15},{10,... | collective-permute-start | bytes 491528 | tf_op jit(solution)/shard_map/ppermute | solution.py:729
  80.1 0.0 collective-permute-done.11.refs_2_
  80.1 1.7 %collective-permute-start.16 = (f32[80,512]{1,0:T(8,128)S(1)}, f32[80,512]{1,0:T(8,128)S(1)}, u32[]{:S(2)}, u32[]{:S(2)}) collective-permute-start(f32[80,512]{1,0:T(8,128)S(1)} %get-tuple-element.55), channel_id=1, source_target_pairs={{0,7},{1,0},{2,1},{3,2},{4,3},{5,4},{6,5},{7,6},{8,15},{9,8},{10,9... | collective-permute-start | bytes 491528 | tf_op jit(solution)/shard_map/ppermute | solution.py:729
  81.9 0.1 collective-permute-done.12.refs_3_
  82.0 15.2 %collective-permute-done.13.refs_4_ = f32[80,512]{1,0:T(8,128)S(1)} collective-permute-done((f32[80,512]{1,0:T(8,128)S(1)}, f32[80,512]{1,0:T(8,128)S(1)}, u32[]{:S(2)}, u32[]{:S(2)}) %collective-permute-start.13) | collective-permute-done | bytes 163872 | tf_op jit(solution)/shard_map/ppermute | solution.py:729
  97.1 0.0 collective-permute-done.14.refs_5_
  97.1 7.6 %collective-permute-done.15.refs_6_ = f32[80,512]{1,0:T(8,128)S(1)} collective-permute-done((f32[80,512]{1,0:T(8,128)S(1)}, f32[80,512]{1,0:T(8,128)S(1)}, u32[]{:S(2)}, u32[]{:S(2)}) %collective-permute-start.15) | collective-permute-done | bytes 163872 | tf_op jit(solution)/shard_map/ppermute | solution.py:729
  104.8 0.1 collective-permute-done.16.refs_7_
  104.8 1.1 %gather_blocks.1 = f32[8,80,512]{2,1,0:T(8,128)} custom-call(f32[80,512]{1,0:T(8,128)S(1)} %get-tuple-element.48.refs_0_, f32[80,512]{1,0:T(8,128)S(1)} %collective-permute-done.10.refs_1_, f32[80,512]{1,0:T(8,128)S(1)} %collective-permute-done.11.refs_2_, f32[80,512]{1,0:T(8,128)S(1)} %collective-permute-done.12.refs_3_, ...), custom_call_target="tpu_custom_call" | custom-call | tf_op jit(solution)/shard_map/gather_blocks/pallas_call | solution.py:690
  (1 shorter events, 0.0 us)
Async XLA Ops:
  3.0 16.3 %collective-permute-start = (f32[3,64,512]{2,1,0:T(8,128)}, f32[3,64,512]{2,1,0:T(8,128)S(1)}, u32[]{:S(2)}, u32[]{:S(2)}) collective-permute-start(f32[3,64,512]{2,1,0:T(8,128)} %get-tuple-element.32), channel_id=1, source_target_pairs={{0,1},{1,0},{2,3},{3,2},{4,5},{5,4},{6,7},{7,6},{8,9},{9,8},{10,11... | collective-permute-start | bytes 1179656 | tf_op jit(solution)/shard_map/ppermute | solution.py:704
  3.7 15.6 %collective-permute-start.1 = (f32[3,64,512]{2,1,0:T(8,128)}, f32[3,64,512]{2,1,0:T(8,128)S(1)}, u32[]{:S(2)}, u32[]{:S(2)}) collective-permute-start(f32[3,64,512]{2,1,0:T(8,128)} %get-tuple-element.33), channel_id=1, source_target_pairs={{0,7},{1,2},{2,1},{3,4},{4,3},{5,6},{6,5},{7,0},{8,15},{9,10},{10,... | collective-permute-start | bytes 1179656 | tf_op jit(solution)/shard_map/ppermute | solution.py:705
  5.0 14.3 %collective-permute-start.2 = (f32[4,104,128]{2,1,0:T(8,128)}, f32[4,104,128]{2,1,0:T(8,128)S(1)}, u32[]{:S(2)}, u32[]{:S(2)}) collective-permute-start(f32[4,104,128]{2,1,0:T(8,128)} %get-tuple-element.34), channel_id=1, source_target_pairs={{0,8},{8,0},{16,24},{24,16},{1,9},{9,1},{17,25},{25,17},{2,10},{10... | collective-permute-start | bytes 638984 | tf_op jit(solution)/shard_map/ppermute | solution.py:704
  5.2 14.0 %collective-permute-start.3 = (f32[4,104,128]{2,1,0:T(8,128)}, f32[4,104,128]{2,1,0:T(8,128)S(1)}, u32[]{:S(2)}, u32[]{:S(2)}) collective-permute-start(f32[4,104,128]{2,1,0:T(8,128)} %get-tuple-element.35), channel_id=1, source_target_pairs={{0,24},{8,16},{16,8},{24,0},{1,25},{9,17},{17,9},{25,1},{2,26},{10... | collective-permute-start | bytes 638984 | tf_op jit(solution)/shard_map/ppermute | solution.py:705
  29.4 19.2 %collective-permute-start.5 = (f32[3,64,512]{2,1,0:T(8,128)S(1)}, f32[3,64,512]{2,1,0:T(8,128)S(1)}, u32[]{:S(2)}, u32[]{:S(2)}) collective-permute-start(f32[3,64,512]{2,1,0:T(8,128)S(1)} %get-tuple-element.41), channel_id=1, source_target_pairs={{0,7},{1,2},{2,1},{3,4},{4,3},{5,6},{6,5},{7,0},{8,15},{9,10},{10,... | collective-permute-start | bytes 1179656 | tf_op jit(solution)/shard_map/ppermute | solution.py:705
  30.6 18.1 %collective-permute-start.4 = (f32[3,64,512]{2,1,0:T(8,128)S(1)}, f32[3,64,512]{2,1,0:T(8,128)S(1)}, u32[]{:S(2)}, u32[]{:S(2)}) collective-permute-start(f32[3,64,512]{2,1,0:T(8,128)S(1)} %get-tuple-element.39.after), channel_id=1, source_target_pairs={{0,1},{1,0},{2,3},{3,2},{4,5},{5,4},{6,7},{7,6},{8,9},{9,8},{10,11... | collective-permute-start | bytes 1179656 | tf_op jit(solution)/shard_map/ppermute | solution.py:704
  30.6 7.1 %collective-permute-start.6 = (f32[4,104,128]{2,1,0:T(8,128)S(1)}, f32[4,104,128]{2,1,0:T(8,128)S(1)}, u32[]{:S(2)}, u32[]{:S(2)}) collective-permute-start(f32[4,104,128]{2,1,0:T(8,128)S(1)} %get-tuple-element.42), channel_id=1, source_target_pairs={{0,8},{8,0},{16,24},{24,16},{1,9},{9,1},{17,25},{25,17},{2,10},{10... | collective-permute-start | bytes 638984 | tf_op jit(solution)/shard_map/ppermute | solution.py:704
  30.8 10.6 %collective-permute-start.7 = (f32[4,104,128]{2,1,0:T(8,128)S(1)}, f32[4,104,128]{2,1,0:T(8,128)S(1)}, u32[]{:S(2)}, u32[]{:S(2)}) collective-permute-start(f32[4,104,128]{2,1,0:T(8,128)S(1)} %get-tuple-element.43), channel_id=1, source_target_pairs={{0,24},{8,16},{16,8},{24,0},{1,25},{9,17},{17,9},{25,1},{2,26},{10... | collective-permute-start | bytes 638984 | tf_op jit(solution)/shard_map/ppermute | solution.py:705
  41.4 7.2 %collective-permute-start.8 = (f32[4,32,128]{2,1,0:T(8,128)S(1)}, f32[4,32,128]{2,1,0:T(8,128)S(1)}, u32[]{:S(2)}, u32[]{:S(2)}) collective-permute-start(f32[4,32,128]{2,1,0:T(8,128)S(1)} %get-tuple-element.45), channel_id=1, source_target_pairs={{0,1},{1,0},{2,3},{3,2},{4,5},{5,4},{6,7},{7,6},{8,9},{9,8},{10,11... | collective-permute-start | bytes 196616 | tf_op jit(solution)/shard_map/ppermute | solution.py:704
  42.8 5.8 %collective-permute-start.9 = (f32[4,32,128]{2,1,0:T(8,128)S(1)}, f32[4,32,128]{2,1,0:T(8,128)S(1)}, u32[]{:S(2)}, u32[]{:S(2)}) collective-permute-start(f32[4,32,128]{2,1,0:T(8,128)S(1)} %get-tuple-element.46), channel_id=1, source_target_pairs={{0,7},{1,2},{2,1},{3,4},{4,3},{5,6},{6,5},{7,0},{8,15},{9,10},{10,... | collective-permute-start | bytes 196616 | tf_op jit(solution)/shard_map/ppermute | solution.py:705
  44.1 4.6 %copy-start = (bf16[512,512]{1,0:T(8,128)(2,1)S(1)}, bf16[512,512]{1,0:T(8,128)(2,1)}, u32[]{:S(2)}) copy-start(bf16[512,512]{1,0:T(8,128)(2,1)} %constant.4.clone.perm_ref) | copy-start | bytes 1572868
  44.1 4.6 %copy-start.1 = (bf16[256,512]{1,0:T(8,128)(2,1)S(1)}, bf16[256,512]{1,0:T(8,128)(2,1)}, u32[]{:S(2)}) copy-start(bf16[256,512]{1,0:T(8,128)(2,1)} %constant.5.clone.zmean_ref) | copy-start | bytes 786436
  44.1 4.6 %copy-start.2 = (s32[1,1,256,1]{2,3,1,0:T(1,128)S(1)}, s32[1,1,256,1]{2,3,1,0:T(1,128)}, u32[]{:S(2)}) copy-start(s32[1,1,256,1]{2,3,1,0:T(1,128)} %param.7) | copy-start | bytes 3076
  69.3 8.5 %collective-permute-start.10 = (f32[80,512]{1,0:T(8,128)S(1)}, f32[80,512]{1,0:T(8,128)S(1)}, u32[]{:S(2)}, u32[]{:S(2)}) collective-permute-start(f32[80,512]{1,0:T(8,128)S(1)} %get-tuple-element.49), channel_id=1, source_target_pairs={{0,1},{1,2},{2,3},{3,4},{4,5},{5,6},{6,7},{7,0},{8,9},{9,10},{10,1... | collective-permute-start | bytes 491528 | tf_op jit(solution)/shard_map/ppermute | solution.py:729
  69.8 10.3 %collective-permute-start.11 = (f32[80,512]{1,0:T(8,128)S(1)}, f32[80,512]{1,0:T(8,128)S(1)}, u32[]{:S(2)}, u32[]{:S(2)}) collective-permute-start(f32[80,512]{1,0:T(8,128)S(1)} %get-tuple-element.50), channel_id=1, source_target_pairs={{0,2},{1,3},{2,4},{3,5},{4,6},{5,7},{6,0},{7,1},{8,10},{9,11},{10,... | collective-permute-start | bytes 491528 | tf_op jit(solution)/shard_map/ppermute | solution.py:729
  72.5 9.5 %collective-permute-start.12 = (f32[80,512]{1,0:T(8,128)S(1)}, f32[80,512]{1,0:T(8,128)S(1)}, u32[]{:S(2)}, u32[]{:S(2)}) collective-permute-start(f32[80,512]{1,0:T(8,128)S(1)} %get-tuple-element.51), channel_id=1, source_target_pairs={{0,3},{1,4},{2,5},{3,6},{4,7},{5,0},{6,1},{7,2},{8,11},{9,12},{10,... | collective-permute-start | bytes 491528 | tf_op jit(solution)/shard_map/ppermute | solution.py:729
  76.1 21.1 %collective-permute-start.13 = (f32[80,512]{1,0:T(8,128)S(1)}, f32[80,512]{1,0:T(8,128)S(1)}, u32[]{:S(2)}, u32[]{:S(2)}) collective-permute-start(f32[80,512]{1,0:T(8,128)S(1)} %get-tuple-element.52), channel_id=1, source_target_pairs={{0,4},{1,5},{2,6},{3,7},{4,0},{5,1},{6,2},{7,3},{8,12},{9,13},{10,... | collective-permute-start | bytes 491528 | tf_op jit(solution)/shard_map/ppermute | solution.py:729
  76.1 21.1 %collective-permute-start.14 = (f32[80,512]{1,0:T(8,128)S(1)}, f32[80,512]{1,0:T(8,128)S(1)}, u32[]{:S(2)}, u32[]{:S(2)}) collective-permute-start(f32[80,512]{1,0:T(8,128)S(1)} %get-tuple-element.53), channel_id=1, source_target_pairs={{0,5},{1,6},{2,7},{3,0},{4,1},{5,2},{6,3},{7,4},{8,13},{9,14},{10,... | collective-permute-start | bytes 491528 | tf_op jit(solution)/shard_map/ppermute | solution.py:729
  77.8 27.0 %collective-permute-start.15 = (f32[80,512]{1,0:T(8,128)S(1)}, f32[80,512]{1,0:T(8,128)S(1)}, u32[]{:S(2)}, u32[]{:S(2)}) collective-permute-start(f32[80,512]{1,0:T(8,128)S(1)} %get-tuple-element.54), channel_id=1, source_target_pairs={{0,6},{1,7},{2,0},{3,1},{4,2},{5,3},{6,4},{7,5},{8,14},{9,15},{10,... | collective-permute-start | bytes 491528 | tf_op jit(solution)/shard_map/ppermute | solution.py:729
  80.1 24.7 %collective-permute-start.16 = (f32[80,512]{1,0:T(8,128)S(1)}, f32[80,512]{1,0:T(8,128)S(1)}, u32[]{:S(2)}, u32[]{:S(2)}) collective-permute-start(f32[80,512]{1,0:T(8,128)S(1)} %get-tuple-element.55), channel_id=1, source_target_pairs={{0,7},{1,0},{2,1},{3,2},{4,3},{5,4},{6,5},{7,6},{8,15},{9,8},{10,9... | collective-permute-start | bytes 491528 | tf_op jit(solution)/shard_map/ppermute | solution.py:729
